TPU v7x, 32 devices: a whole 2x2x4 slice. The times are simulated.
32 devices in a mesh: groups: 2 (over x), slab: 16 (over z, y, core).
Axes of the slice: x: 2, y: 2, z: 4, core: 2. Of those that a mesh axis runs over, the one named last changes fastest.
Arguments:
- activations: bfloat16 [2048, 65536], P(('groups', 'slab')), parts along dimension 0, may hold values from 0 to 4
- weights: bfloat16 [6, 2, 512, 128, 128], P(None, None, 'slab'), may hold values from -0.5 to 0.5
- biases: float32 [6, 65536], P(None, 'slab'), may hold values from -1 to 0.5
- columns: int32 [6, 512], P(None, 'slab'), may hold values from 0 to 31
Outputs:
- features: bfloat16 [2048, 65536], P(('groups', 'slab')), parts along dimension 0
There are 2 independent parts, one for each index of `groups`. A program takes and returns all parts, laid end to end along the dimension named above; an argument that names none is the same for every part. Nothing has to cross between parts.
Inputs may be any that keep to these rules, and one draw needn't show every extreme that they name: columns name a block within a group of 32 consecutive blocks.
All inputs are finite; a program needn't handle non-finite values.
Results may differ from a plain program's by a relative error of at most 0.0072.
Values may be sent and summed in bfloat16 or wider, within the bound.
No kernel may reach another device: no remote copies, remote signals or barrier semaphores. Data moves between devices by JAX's collectives and lax.ppermute only.
A program may use at most 128 MiB of HBM per device.

v0:
```python
import functools

import jax
import jax.numpy as jnp
from jax import lax
from jax.experimental import pallas as pl
from jax.experimental.pallas import tpu as pltpu
from jax.sharding import PartitionSpec as P


ceiling = 4.0


def swap(block, axis, offset):
    count = lax.axis_size(axis)
    return lax.ppermute(block, axis, [(i, i ^ offset) for i in range(count)])


def section_bit(section, remote, log_count):
    if remote <= 1:
        return log_count - 1
    return (remote - 1 - section) * (log_count - 1) // (remote - 1)


def split_kernel(offsets, first_bit, me_ref, act_ref, *refs):
    count = len(offsets)
    outs, taken, sems = refs[:count], refs[count], refs[count + 1]
    width = taken.shape[-1]
    half = pl.program_id(0)

    def copy(h, j):
        home = me_ref[0] ^ (offsets[j] | (h << first_bit))
        start = pl.multiple_of(home * width, 128)
        return pltpu.make_async_copy(
            act_ref.at[:, pl.ds(start, width)], taken.at[h, j], sems.at[h, j]
        )

    @pl.when(half == 0)
    def _():
        for h in range(2):
            for j in range(count):
                copy(h, j).start()

    for j in range(count):
        copy(half, j).wait()
        for k in range(width // 128):
            outs[j][0, k] = taken[half, j, :, k * 128 : (k + 1) * 128]


def split(me, activations, offsets, first_bit, blocks):
    rows = activations.shape[0]
    count = len(offsets)
    width = blocks * 128
    piece = jax.ShapeDtypeStruct((2, blocks, rows, 128), activations.dtype)
    return pl.pallas_call(
        functools.partial(split_kernel, offsets, first_bit),
        out_shape=[piece] * count,
        grid_spec=pltpu.PrefetchScalarGridSpec(
            num_scalar_prefetch=1,
            grid=(2,),
            in_specs=[pl.BlockSpec(memory_space=pl.ANY)],
            out_specs=[pl.BlockSpec((1, blocks, rows, 128), lambda h, me: (h, 0, 0, 0))] * count,
            scratch_shapes=[
                pltpu.VMEM((2, count, rows, width), activations.dtype),
                pltpu.SemaphoreType.DMA((2, count)),
            ],
        ),
        cost_estimate=pl.CostEstimate(
            flops=0, transcendentals=0, bytes_accessed=4 * activations.size
        ),
        name="split",
    )(me, activations)


def merge_kernel(offsets, half_bit, aliased, me_ref, *refs):
    count = len(offsets)
    pieces = refs[:count]
    out_ref, placed, sems = refs[count + aliased :]
    width = placed.shape[-1]
    step = pl.program_id(0)
    last = pl.num_programs(0) - 1
    rows = placed.shape[-2]

    def copy(at, j):
        home = me_ref[0] ^ (offsets[j] | half_bit)
        start = pl.multiple_of(home * width, 128)
        return pltpu.make_async_copy(
            placed.at[at, j],
            out_ref.at[pl.ds(at * rows, rows), pl.ds(start, width)],
            sems.at[at, j],
        )

    for j in range(count):
        for k in range(width // 128):
            placed[step, j, :, k * 128 : (k + 1) * 128] = pieces[j][k]
        copy(step, j).start()

    @pl.when(step == last)
    def _():
        for at in range(placed.shape[0]):
            for j in range(count):
                copy(at, j).wait()


def merge(me, pieces, offsets, half_bit, into):
    count = len(offsets)
    blocks, total_rows, _ = pieces[0].shape
    steps = 2 if total_rows % 32 == 0 else 1
    rows = total_rows // steps
    width = blocks * 128
    aliased = 0 if into is None else 1
    more = [] if into is None else [into]
    return pl.pallas_call(
        functools.partial(merge_kernel, offsets, half_bit, aliased),
        out_shape=jax.ShapeDtypeStruct((total_rows, 2 * count * width), pieces[0].dtype),
        grid_spec=pltpu.PrefetchScalarGridSpec(
            num_scalar_prefetch=1,
            grid=(steps,),
            in_specs=[pl.BlockSpec((blocks, rows, 128), lambda i, me: (0, i, 0))] * count
            + [pl.BlockSpec(memory_space=pl.ANY)] * aliased,
            out_specs=pl.BlockSpec(memory_space=pl.ANY),
            scratch_shapes=[
                pltpu.VMEM((steps, count, rows, width), pieces[0].dtype),
                pltpu.SemaphoreType.DMA((steps, count)),
            ],
        ),
        input_output_aliases={1 + count: 0} if aliased else {},
        cost_estimate=pl.CostEstimate(
            flops=0, transcendentals=0, bytes_accessed=4 * count * pieces[0].size
        ),
    )(me, *pieces, *more)


def layers_kernel(plan, cols_ref, me_ref, *refs):
    sources, half, flip, joined_out, step, layer, blocks = plan
    refs = list(refs)
    src = [refs.pop(0) for _ in range(sources)]
    other = refs.pop(0) if sources == 1 else None
    w = [[refs.pop(0), refs.pop(0)] for _ in range(2)]
    bias = refs.pop(0)
    middle = refs.pop()
    outs = refs
    phase, at = pl.program_id(0), pl.program_id(1)
    count, _, rows, _ = middle.shape

    def whole(ref, k):
        return ref[:, k].reshape(count * rows, 128)

    def from_source(k):
        if sources == 1:
            return whole(src[0], k)
        return jnp.concatenate([piece[half, k] for piece in src], axis=0)

    def from_partner(k):
        if sources > 1:
            return jnp.concatenate([piece[1 - half, k] for piece in src], axis=0)
        return jnp.concatenate([other[j ^ flip, k] for j in range(count)], axis=0)

    def from_middle(k):
        return whole(middle, k)

    def run(p, own_of, partner_of, store):
        for t in range(step):
            k = at * step + t
            c = cols_ref[((layer + p) * 2 + half) * blocks + k]
            both = jnp.concatenate([own_of(k), partner_of(c)], axis=1)
            taken = jnp.concatenate([w[p][0][0, t], w[p][1][0, t]], axis=0)
            summed = jnp.dot(both, taken, preferred_element_type=jnp.float32)
            summed = summed + bias[0, 0, t]
            store(k, t, jnp.clip(summed, 0.0, ceiling).astype(jnp.bfloat16))

    @pl.when(phase == 0)
    def _():
        def store(k, t, value):
            middle[:, k] = value.reshape(count, rows, 128)

        run(0, from_source, from_partner, store)

    @pl.when(phase == 1)
    def _():
        def store(k, t, value):
            if joined_out:
                outs[0][:, t] = value.reshape(count, rows, 128)
            else:
                for j in range(count):
                    outs[j][t] = value[j * rows : (j + 1) * rows]

        run(1, from_middle, from_middle, store)


def two_layers(
    cols, me, source, other, weights, far, biases, layer, half, rows, count, flip, joined_out
):
    blocks = biases.shape[2]
    part = weights.shape[2]
    step = min(8, part, blocks)
    steps = blocks // step

    def weight_spec(p, which):
        def index(phase, at, cols, me):
            at = jnp.where(phase == p, at, (steps - 1) if p == 0 else 0)
            first = which * blocks + at * step
            piece, row = first // part, (first % part) // step
            if half == 0:
                return (layer + p, piece * (part // step) + row, 0, 0)
            return (far[p][1], (piece ^ me[1]) * (part // step) + row, 0, 0)

        return pl.BlockSpec((1, step, 128, 128), index)

    if other is None:
        specs = [pl.BlockSpec((2, blocks, rows, 128), lambda p, a, c, m: (0, 0, 0, 0))] * count
        operands = list(source)
    else:
        specs = [pl.BlockSpec((count, blocks, rows, 128), lambda p, a, c, m: (0, 0, 0, 0))] * 2
        operands = [source, other]
    own = weights.reshape(weights.shape[0], 2 * blocks, 128, 128)
    for p in range(2):
        for which in range(2):
            specs.append(weight_spec(p, which))
            operands.append(own if half == 0 else far[p][0])
    specs.append(pl.BlockSpec((1, 1, step, 1, 128), lambda p, a, c, m: (layer + p, half, a, 0, 0)))
    operands.append(biases)
    if joined_out:
        out_shape = jax.ShapeDtypeStruct((count, blocks, rows, 128), jnp.bfloat16)
        out_specs = pl.BlockSpec((count, step, rows, 128), lambda p, a, c, m: (0, a * p, 0, 0))
    else:
        out_shape = [jax.ShapeDtypeStruct((blocks, rows, 128), jnp.bfloat16)] * count
        out_specs = [pl.BlockSpec((step, rows, 128), lambda p, a, c, m: (a * p, 0, 0))] * count
    plan = (1 if other is not None else count, half, flip, joined_out, step, layer, blocks)
    cells = count * rows * blocks
    return pl.pallas_call(
        functools.partial(layers_kernel, plan),
        out_shape=out_shape,
        grid_spec=pltpu.PrefetchScalarGridSpec(
            num_scalar_prefetch=2,
            grid=(2, steps),
            in_specs=specs,
            out_specs=out_specs,
            scratch_shapes=[pltpu.VMEM((count, blocks, rows, 128), jnp.bfloat16)],
        ),
        cost_estimate=pl.CostEstimate(
            flops=2 * 2 * cells * 256 * 128,
            transcendentals=0,
            bytes_accessed=2 * 3 * cells * 128 + 2 * 2 * blocks * 128 * 128 * 2,
        ),
    )(cols, me, *operands)


def far_batches(layer_count):
    return [(l, 2) for l in range(0, layer_count - 2, 2)] + [
        (layer_count - 2, 1),
        (layer_count - 1, 1),
    ]


def local(activations, weights, biases, columns):
    slab_count, group_count = lax.axis_size("slab"), lax.axis_size("groups")
    log_count = slab_count.bit_length() - 1
    layer_count, _, blocks, width, _ = weights.shape
    rows = activations.shape[0]
    remote = (layer_count + 1) // 2
    bits = [section_bit(m, remote, log_count) for m in range(remote)]
    first_bit = bits[0]
    spread = [b for b in range(log_count) if b != first_bit]
    count = slab_count // 2
    offsets = [
        sum(((j >> i) & 1) << b for i, b in enumerate(spread)) for j in range(count)
    ]
    slab, group = lax.axis_index("slab"), lax.axis_index("groups")
    me = jnp.stack([slab, group]).astype(jnp.int32)

    mine = split(me, activations, offsets, first_bit, blocks)
    pieces = [mine[0]]
    for j in range(1, count):
        pieces.append(swap(mine[j], "slab", offsets[j]))

    far_bias = swap(biases, "slab", 1 << first_bit)
    far_columns = swap(columns, "slab", 1 << first_bit)
    bias = jnp.stack([biases, far_bias], axis=1).reshape(layer_count, 2, blocks, 1, width)
    cols = jnp.stack([columns, far_columns], axis=1).reshape(-1)

    part = 2 * blocks // group_count
    parts = weights.reshape(layer_count, group_count, part, width, width)
    far = []
    for first, size in far_batches(layer_count):
        part_mine = lax.dynamic_slice(
            parts, (first, group, 0, 0, 0), (size, 1, part, width, width)
        ).reshape(size, part, width, width)
        held = [swap(part_mine, "slab", 1 << first_bit)]
        for b in range(group_count.bit_length() - 1):
            got = []
            for one in held:
                got.append(swap(one, "groups", 1 << b))
            held = held + got
        joined = jnp.concatenate(held, axis=1)
        far += [(joined, i) for i in range(size)]

    def weights_of(half, layer):
        return [None, None] if half == 0 else far[layer : layer + 2]

    halves = [pieces, pieces]
    for m in range(remote):
        last = m == remote - 1
        for half in range(2):
            other, flip = None, 0
            if m > 0:
                other = swap(halves[half], "slab", 1 << bits[m])
                flip = offsets.index(1 << bits[m])
            halves[half] = two_layers(
                cols, me, halves[half], other, parts, weights_of(half, 2 * m), bias,
                2 * m, half, rows, count, flip, not last,
            )
    output = None
    for half in range(2):
        back = [halves[half][0]]
        for j in range(1, count):
            back.append(swap(halves[half][j], "slab", offsets[j]))
        output = merge(me, back, offsets, half << first_bit, output)
    return output


def solution(mesh):
    placed = (
        P(("groups", "slab"), None),
        P(None, None, "slab", None, None),
        P(None, "slab"),
        P(None, "slab"),
    )

    return jax.shard_map(
        local, mesh=mesh, in_specs=placed, out_specs=P(("groups", "slab"), None), check_vma=False
    )
```

profile of v0, /device:TPU:1, one launch (start us, length us, event | category | flops | bytes accessed | tf_op | source)
XLA Modules:
  0.0 629.3 jit_solution(5129551584266635065)
XLA Ops:
  0.0 4.8 dynamic-slice_bitcast_fusion
  8.6 7.3 %split.1 = (bf16[2,32,64,128]{3,2,1,0:T(8,128)(2,1)}, bf16[2,32,64,128]{3,2,1,0:T(8,128)(2,1)}, bf16[2,32,64,128]{3,2,1,0:T(8,128)(2,1)}, bf16[2,32,64,128]{3,2,...) custom-call(s32[2]{0:T(128)} %pad_add_fusion.1.me_ref, ...), custom_call_target="tpu_custom_call" | custom-call | bytes 16777216 | tf_op jit(solution)/shard_map/split/pallas_call | solution.py:55
  18.6 79.9 %collective-permute-done.8 = bf16[2,32,128,128]{3,2,1,0:T(8,128)(2,1)} collective-permute-done((bf16[2,32,128,128]{3,2,1,0:T(8,128)(2,1)}, bf16[2,32,128,128]{3,2,1,0:T(8,128)(2,1)}, u32[]{:S(2)}, u32[]{:S(2)}) %collective-permute-start.8) | collective-permute-done | bytes 2097184 | tf_op jit(solution)/shard_map/ppermute | solution.py:16
  99.5 3.4 collective-permute-done
  102.9 4.7 collective-permute-done.10
  110.5 4.3 collective-permute-start.5
  117.9 13.1 %collective-permute-done.4.refs_4_ = bf16[2,32,64,128]{3,2,1,0:T(8,128)(2,1)} collective-permute-done((bf16[2,32,64,128]{3,2,1,0:T(8,128)(2,1)}, bf16[2,32,64,128]{3,2,1,0:T(8,128)(2,1)}, u32[]{:S(2)}, u32[]{:S(2)}) %collective-permute-start.4) | collective-permute-done | bytes 1048608 | tf_op jit(solution)/shard_map/ppermute | solution.py:16
  131.0 30.4 %collective-permute-done.5.refs_5_ = bf16[2,32,64,128]{3,2,1,0:T(8,128)(2,1)} collective-permute-done((bf16[2,32,64,128]{3,2,1,0:T(8,128)(2,1)}, bf16[2,32,64,128]{3,2,1,0:T(8,128)(2,1)}, u32[]{:S(2)}, u32[]{:S(2)}) %collective-permute-start.5) | collective-permute-done | bytes 1048608 | tf_op jit(solution)/shard_map/ppermute | solution.py:16
  161.3 15.5 %collective-permute-done.6.refs_6_ = bf16[2,32,64,128]{3,2,1,0:T(8,128)(2,1)} collective-permute-done((bf16[2,32,64,128]{3,2,1,0:T(8,128)(2,1)}, bf16[2,32,64,128]{3,2,1,0:T(8,128)(2,1)}, u32[]{:S(2)}, u32[]{:S(2)}) %collective-permute-start.6) | collective-permute-done | bytes 1048608 | tf_op jit(solution)/shard_map/ppermute | solution.py:16
  176.9 26.3 %collective-permute-done.7.refs_7_ = bf16[2,32,64,128]{3,2,1,0:T(8,128)(2,1)} collective-permute-done((bf16[2,32,64,128]{3,2,1,0:T(8,128)(2,1)}, bf16[2,32,64,128]{3,2,1,0:T(8,128)(2,1)}, u32[]{:S(2)}, u32[]{:S(2)}) %collective-permute-start.7) | collective-permute-done | bytes 1048608 | tf_op jit(solution)/shard_map/ppermute | solution.py:16
  203.2 13.2 %shard_map.49.refs_0_ = bf16[8,32,64,128]{3,2,1,0:T(8,128)(2,1)} custom-call(s32[384]{0:T(512)} %reshape.25.cols_ref, s32[2]{0:T(128)} %pad_add_fusion.1.me_ref, bf16[2,32,64,128]{3,2,1,0:T(8,128)(2,1)} %get-tuple-element.29.refs_0_, bf16[2,32,64,128]{3,2,1,0:T(8,128)(2,1)} %copy-done.1, bf16[2,32,64,128]{3,2,1,0:T(8,128)(2,1)} %copy-done.2, ...), custom_call_target="tpu_custom_call" | custom-call | flops 2147483648 | bytes 16777216 | tf_op jit(solution)/shard_map/pallas_call | solution.py:231
  219.2 4.6 pad_maximum_fusion.refs_8_.refs_9_.refs_10_.refs_11_
  223.8 13.2 %shard_map.46.refs_0_ = bf16[8,32,64,128]{3,2,1,0:T(8,128)(2,1)} custom-call(s32[384]{0:T(512)} %reshape.25.cols_ref, s32[2]{0:T(128)} %pad_add_fusion.1.me_ref, bf16[2,32,64,128]{3,2,1,0:T(8,128)(2,1)} %get-tuple-element.29.refs_0_, bf16[2,32,64,128]{3,2,1,0:T(8,128)(2,1)} %copy-done.1, bf16[2,32,64,128]{3,2,1,0:T(8,128)(2,1)} %copy-done.2, ...), custom_call_target="tpu_custom_call" | custom-call | flops 2147483648 | bytes 16777216 | tf_op jit(solution)/shard_map/pallas_call | solution.py:231
  238.2 72.0 %collective-permute-done.12 = bf16[2,32,128,128]{3,2,1,0:T(8,128)(2,1)S(1)} collective-permute-done((bf16[2,32,128,128]{3,2,1,0:T(8,128)(2,1)}, bf16[2,32,128,128]{3,2,1,0:T(8,128)(2,1)S(1)}, u32[]{:S(2)}, u32[]{:S(2)}) %collective-permute-start.12) | collective-permute-done | bytes 2097184 | tf_op jit(solution)/shard_map/ppermute | solution.py:16
  310.2 13.2 %shard_map.50.refs_0_ = bf16[8,32,64,128]{3,2,1,0:T(8,128)(2,1)} custom-call(s32[384]{0:T(512)} %reshape.25.cols_ref, s32[2]{0:T(128)} %pad_add_fusion.1.me_ref, bf16[8,32,64,128]{3,2,1,0:T(8,128)(2,1)} %shard_map.49.refs_0_, bf16[8,32,64,128]{3,2,1,0:T(8,128)(2,1)} %collective-permute-done.26.refs_1_, bf16[6,64,128,128]{3,2,1,0:T(8,128)(2,1)} %bitcast.17, ...), custom_call_target="tpu_custom_call" | custom-call | flops 2147483648 | bytes 16777216 | tf_op jit(solution)/shard_map/pallas_call | solution.py:231
  324.5 32.3 %collective-permute-done.13 = bf16[2,32,128,128]{3,2,1,0:T(8,128)(2,1)} collective-permute-done((bf16[2,32,128,128]{3,2,1,0:T(8,128)(2,1)S(1)}, bf16[2,32,128,128]{3,2,1,0:T(8,128)(2,1)}, u32[]{:S(2)}, u32[]{:S(2)}) %collective-permute-start.13) | collective-permute-done | bytes 2097184 | tf_op jit(solution)/shard_map/ppermute | solution.py:16
  356.8 4.0 pad_maximum_fusion.1.refs_2_.refs_3_.refs_4_.refs_5_
  360.7 37.1 %collective-permute-done.11.refs_1_ = bf16[8,32,64,128]{3,2,1,0:T(8,128)(2,1)} collective-permute-done((bf16[8,32,64,128]{3,2,1,0:T(8,128)(2,1)}, bf16[8,32,64,128]{3,2,1,0:T(8,128)(2,1)}, u32[]{:S(2)}, u32[]{:S(2)}) %collective-permute-start.11) | collective-permute-done | bytes 4194336 | tf_op jit(solution)/shard_map/ppermute | solution.py:16
  397.8 13.2 %shard_map.47.refs_0_ = bf16[8,32,64,128]{3,2,1,0:T(8,128)(2,1)} custom-call(s32[384]{0:T(512)} %reshape.25.cols_ref, s32[2]{0:T(128)} %pad_add_fusion.1.me_ref, bf16[8,32,64,128]{3,2,1,0:T(8,128)(2,1)} %shard_map.46.refs_0_, bf16[8,32,64,128]{3,2,1,0:T(8,128)(2,1)} %collective-permute-done.11.refs_1_, ...), custom_call_target="tpu_custom_call" | custom-call | flops 2147483648 | bytes 16777216 | tf_op jit(solution)/shard_map/pallas_call | solution.py:231
  416.1 68.0 %collective-permute-done.15 = bf16[1,32,128,128]{3,2,1,0:T(8,128)(2,1)S(1)} collective-permute-done((bf16[1,32,128,128]{3,2,1,0:T(8,128)(2,1)S(1)}, bf16[1,32,128,128]{3,2,1,0:T(8,128)(2,1)S(1)}, u32[]{:S(2)}, u32[]{:S(2)}) %collective-permute-start.15) | collective-permute-done | bytes 1048608 | tf_op jit(solution)/shard_map/ppermute | solution.py:16
  484.1 22.5 %collective-permute-done.17 = bf16[1,32,128,128]{3,2,1,0:T(8,128)(2,1)S(1)} collective-permute-done((bf16[1,32,128,128]{3,2,1,0:T(8,128)(2,1)S(1)}, bf16[1,32,128,128]{3,2,1,0:T(8,128)(2,1)S(1)}, u32[]{:S(2)}, u32[]{:S(2)}) %collective-permute-start.17) | collective-permute-done | bytes 1048608 | tf_op jit(solution)/shard_map/ppermute | solution.py:16
  506.6 13.2 %shard_map.51 = (bf16[32,64,128]{2,1,0:T(8,128)(2,1)}, bf16[32,64,128]{2,1,0:T(8,128)(2,1)}, bf16[32,64,128]{2,1,0:T(8,128)(2,1)}, bf16[32,64,128]{2,1,0:T(8,128...) custom-call(s32[384]{0:T(512)} %reshape.25.cols_ref, ...), custom_call_target="tpu_custom_call" | custom-call | flops 2147483648 | bytes 16777216 | tf_op jit(solution)/shard_map/pallas_call | solution.py:231
  522.7 7.8 %collective-permute-done.18 = bf16[1,32,128,128]{3,2,1,0:T(8,128)(2,1)} collective-permute-done((bf16[1,32,128,128]{3,2,1,0:T(8,128)(2,1)S(1)}, bf16[1,32,128,128]{3,2,1,0:T(8,128)(2,1)}, u32[]{:S(2)}, u32[]{:S(2)}) %collective-permute-start.18) | collective-permute-done | bytes 1048608 | tf_op jit(solution)/shard_map/ppermute | solution.py:16
  538.1 13.4 %shard_map.48 = (bf16[32,64,128]{2,1,0:T(8,128)(2,1)}, bf16[32,64,128]{2,1,0:T(8,128)(2,1)}, bf16[32,64,128]{2,1,0:T(8,128)(2,1)}, bf16[32,64,128]{2,1,0:T(8,128...) custom-call(s32[384]{0:T(512)} %reshape.25.cols_ref, ...), custom_call_target="tpu_custom_call" | custom-call | flops 2147483648 | bytes 16777216 | tf_op jit(solution)/shard_map/pallas_call | solution.py:231
  557.4 9.6 %collective-permute-done.33.refs_6_ = bf16[32,64,128]{2,1,0:T(8,128)(2,1)S(1)} collective-permute-done((bf16[32,64,128]{2,1,0:T(8,128)(2,1)}, bf16[32,64,128]{2,1,0:T(8,128)(2,1)S(1)}, u32[]{:S(2)}, u32[]{:S(2)}) %collective-permute-start.33) | collective-permute-done | bytes 524320 | tf_op jit(solution)/shard_map/ppermute | solution.py:16
  567.3 14.1 %collective-permute-done.34.refs_7_ = bf16[32,64,128]{2,1,0:T(8,128)(2,1)S(1)} collective-permute-done((bf16[32,64,128]{2,1,0:T(8,128)(2,1)}, bf16[32,64,128]{2,1,0:T(8,128)(2,1)S(1)}, u32[]{:S(2)}, u32[]{:S(2)}) %collective-permute-start.34) | collective-permute-done | bytes 524320 | tf_op jit(solution)/shard_map/ppermute | solution.py:16
  581.5 8.5 %collective-permute-done.20.refs_2_ = bf16[32,64,128]{2,1,0:T(8,128)(2,1)S(1)} collective-permute-done((bf16[32,64,128]{2,1,0:T(8,128)(2,1)}, bf16[32,64,128]{2,1,0:T(8,128)(2,1)S(1)}, u32[]{:S(2)}, u32[]{:S(2)}) %collective-permute-start.20) | collective-permute-done | bytes 524320 | tf_op jit(solution)/shard_map/ppermute | solution.py:16
  590.9 4.4 shard_map.52.refs_8_
  595.4 6.5 %collective-permute-done.21.refs_3_ = bf16[32,64,128]{2,1,0:T(8,128)(2,1)S(1)} collective-permute-done((bf16[32,64,128]{2,1,0:T(8,128)(2,1)}, bf16[32,64,128]{2,1,0:T(8,128)(2,1)S(1)}, u32[]{:S(2)}, u32[]{:S(2)}) %collective-permute-start.21) | collective-permute-done | bytes 524320 | tf_op jit(solution)/shard_map/ppermute | solution.py:16
  601.9 10.2 %collective-permute-done.24.refs_6_ = bf16[32,64,128]{2,1,0:T(8,128)(2,1)} collective-permute-done((bf16[32,64,128]{2,1,0:T(8,128)(2,1)}, bf16[32,64,128]{2,1,0:T(8,128)(2,1)}, u32[]{:S(2)}, u32[]{:S(2)}) %collective-permute-start.24) | collective-permute-done | bytes 524320 | tf_op jit(solution)/shard_map/ppermute | solution.py:16
  612.0 12.7 %collective-permute-done.25.refs_7_ = bf16[32,64,128]{2,1,0:T(8,128)(2,1)} collective-permute-done((bf16[32,64,128]{2,1,0:T(8,128)(2,1)}, bf16[32,64,128]{2,1,0:T(8,128)(2,1)}, u32[]{:S(2)}, u32[]{:S(2)}) %collective-permute-start.25) | collective-permute-done | bytes 524320 | tf_op jit(solution)/shard_map/ppermute | solution.py:16
  624.7 4.4 shard_map.53
  (87 shorter events, 41.3 us)
Async XLA Ops:
  4.8 93.7 %collective-permute-start.8 = (bf16[2,32,128,128]{3,2,1,0:T(8,128)(2,1)}, bf16[2,32,128,128]{3,2,1,0:T(8,128)(2,1)}, u32[]{:S(2)}, u32[]{:S(2)}) collective-permute-start(bf16[2,32,128,128]{3,2,1,0:T(8,128)(2,1)} %get-tuple-element.56), channel_id=1, source_target_pairs={{0,8},{1,9},{2,10},{3,11},{4,12},{5,13},{6,14},{7,15},{8,0},{9,1},... | collective-permute-start | bytes 6291464 | tf_op jit(solution)/shard_map/ppermute | solution.py:16
  15.9 94.6 %collective-permute-start.1 = (bf16[2,32,64,128]{3,2,1,0:T(8,128)(2,1)}, bf16[2,32,64,128]{3,2,1,0:T(8,128)(2,1)S(1)}, u32[]{:S(2)}, u32[]{:S(2)}) collective-permute-start(bf16[2,32,64,128]{3,2,1,0:T(8,128)(2,1)} %get-tuple-element.30), channel_id=1, source_target_pairs={{0,1},{1,0},{2,3},{3,2},{4,5},{5,4},{6,7},{7,6},{8,9},{9,8},{10,11... | collective-permute-start | bytes 3145736 | tf_op jit(solution)/shard_map/ppermute | solution.py:16
  16.9 97.9 %collective-permute-start.2 = (bf16[2,32,64,128]{3,2,1,0:T(8,128)(2,1)}, bf16[2,32,64,128]{3,2,1,0:T(8,128)(2,1)S(1)}, u32[]{:S(2)}, u32[]{:S(2)}) collective-permute-start(bf16[2,32,64,128]{3,2,1,0:T(8,128)(2,1)} %get-tuple-element.31), channel_id=1, source_target_pairs={{0,2},{1,3},{2,0},{3,1},{4,6},{5,7},{6,4},{7,5},{8,10},{9,11},{10,... | collective-permute-start | bytes 3145736 | tf_op jit(solution)/shard_map/ppermute | solution.py:16
  18.2 97.5 %collective-permute-start.3 = (bf16[2,32,64,128]{3,2,1,0:T(8,128)(2,1)}, bf16[2,32,64,128]{3,2,1,0:T(8,128)(2,1)S(1)}, u32[]{:S(2)}, u32[]{:S(2)}) collective-permute-start(bf16[2,32,64,128]{3,2,1,0:T(8,128)(2,1)} %get-tuple-element.32), channel_id=1, source_target_pairs={{0,3},{1,2},{2,1},{3,0},{4,7},{5,6},{6,5},{7,4},{8,11},{9,10},{10,... | collective-permute-start | bytes 3145736 | tf_op jit(solution)/shard_map/ppermute | solution.py:16
  98.5 120.7 %collective-permute-start.9 = (bf16[2,32,128,128]{3,2,1,0:T(8,128)(2,1)}, bf16[2,32,128,128]{3,2,1,0:T(8,128)(2,1)}, u32[]{:S(2)}, u32[]{:S(2)}) collective-permute-start(bf16[2,32,128,128]{3,2,1,0:T(8,128)(2,1)} %collective-permute-done.8), channel_id=1, source_target_pairs={{0,16},{16,0},{1,17},{17,1},{2,18},{18,2},{3,19},{19,3},{4,20},{20... | collective-permute-start | bytes 6291464 | tf_op jit(solution)/shard_map/ppermute | solution.py:16
  107.6 23.4 %collective-permute-start.4 = (bf16[2,32,64,128]{3,2,1,0:T(8,128)(2,1)}, bf16[2,32,64,128]{3,2,1,0:T(8,128)(2,1)}, u32[]{:S(2)}, u32[]{:S(2)}) collective-permute-start(bf16[2,32,64,128]{3,2,1,0:T(8,128)(2,1)} %get-tuple-element.33), channel_id=1, source_target_pairs={{0,4},{1,5},{2,6},{3,7},{4,0},{5,1},{6,2},{7,3},{8,12},{9,13},{10,... | collective-permute-start | bytes 3145736 | tf_op jit(solution)/shard_map/ppermute | solution.py:16
  110.5 50.8 %collective-permute-start.5 = (bf16[2,32,64,128]{3,2,1,0:T(8,128)(2,1)}, bf16[2,32,64,128]{3,2,1,0:T(8,128)(2,1)}, u32[]{:S(2)}, u32[]{:S(2)}) collective-permute-start(bf16[2,32,64,128]{3,2,1,0:T(8,128)(2,1)} %get-tuple-element.34), channel_id=1, source_target_pairs={{0,5},{1,4},{2,7},{3,6},{4,1},{5,0},{6,3},{7,2},{8,13},{9,12},{10,... | collective-permute-start | bytes 3145736 | tf_op jit(solution)/shard_map/ppermute | solution.py:16
  114.9 62.0 %collective-permute-start.6 = (bf16[2,32,64,128]{3,2,1,0:T(8,128)(2,1)}, bf16[2,32,64,128]{3,2,1,0:T(8,128)(2,1)}, u32[]{:S(2)}, u32[]{:S(2)}) collective-permute-start(bf16[2,32,64,128]{3,2,1,0:T(8,128)(2,1)} %get-tuple-element.35), channel_id=1, source_target_pairs={{0,6},{1,7},{2,4},{3,5},{4,2},{5,3},{6,0},{7,1},{8,14},{9,15},{10,... | collective-permute-start | bytes 3145736 | tf_op jit(solution)/shard_map/ppermute | solution.py:16
  115.6 87.5 %collective-permute-start.7 = (bf16[2,32,64,128]{3,2,1,0:T(8,128)(2,1)}, bf16[2,32,64,128]{3,2,1,0:T(8,128)(2,1)}, u32[]{:S(2)}, u32[]{:S(2)}) collective-permute-start(bf16[2,32,64,128]{3,2,1,0:T(8,128)(2,1)} %get-tuple-element.36), channel_id=1, source_target_pairs={{0,7},{1,6},{2,5},{3,4},{4,3},{5,2},{6,1},{7,0},{8,15},{9,14},{10,... | collective-permute-start | bytes 3145736 | tf_op jit(solution)/shard_map/ppermute | solution.py:16
  216.4 93.8 %collective-permute-start.26 = (bf16[8,32,64,128]{3,2,1,0:T(8,128)(2,1)}, bf16[8,32,64,128]{3,2,1,0:T(8,128)(2,1)}, u32[]{:S(2)}, u32[]{:S(2)}) collective-permute-start(bf16[8,32,64,128]{3,2,1,0:T(8,128)(2,1)} %shard_map.49.refs_0_), channel_id=1, source_target_pairs={{0,2},{1,3},{2,0},{3,1},{4,6},{5,7},{6,4},{7,5},{8,10},{9,11},{10,... | collective-permute-start | bytes 12582920 | tf_op jit(solution)/shard_map/ppermute | solution.py:16
  216.6 93.6 %collective-permute-start.12 = (bf16[2,32,128,128]{3,2,1,0:T(8,128)(2,1)}, bf16[2,32,128,128]{3,2,1,0:T(8,128)(2,1)S(1)}, u32[]{:S(2)}, u32[]{:S(2)}) collective-permute-start(bf16[2,32,128,128]{3,2,1,0:T(8,128)(2,1)} %get-tuple-element.55), channel_id=1, source_target_pairs={{0,8},{1,9},{2,10},{3,11},{4,12},{5,13},{6,14},{7,15},{8,0},{9,1},... | collective-permute-start | bytes 6291464 | tf_op jit(solution)/shard_map/ppermute | solution.py:16
  237.0 160.8 %collective-permute-start.11 = (bf16[8,32,64,128]{3,2,1,0:T(8,128)(2,1)}, bf16[8,32,64,128]{3,2,1,0:T(8,128)(2,1)}, u32[]{:S(2)}, u32[]{:S(2)}) collective-permute-start(bf16[8,32,64,128]{3,2,1,0:T(8,128)(2,1)} %shard_map.46.refs_0_), channel_id=1, source_target_pairs={{0,2},{1,3},{2,0},{3,1},{4,6},{5,7},{6,4},{7,5},{8,10},{9,11},{10,... | collective-permute-start | bytes 12582920 | tf_op jit(solution)/shard_map/ppermute | solution.py:16
  310.2 46.6 %collective-permute-start.13 = (bf16[2,32,128,128]{3,2,1,0:T(8,128)(2,1)S(1)}, bf16[2,32,128,128]{3,2,1,0:T(8,128)(2,1)}, u32[]{:S(2)}, u32[]{:S(2)}) collective-permute-start(bf16[2,32,128,128]{3,2,1,0:T(8,128)(2,1)S(1)} %collective-permute-done.12), channel_id=1, source_target_pairs={{0,16},{16,0},{1,17},{17,1},{2,18},{18,2},{3,19},{19,3},{4,20},{20... | collective-permute-start | bytes 6291464 | tf_op jit(solution)/shard_map/ppermute | solution.py:16
  323.4 183.2 %collective-permute-start.27 = (bf16[8,32,64,128]{3,2,1,0:T(8,128)(2,1)}, bf16[8,32,64,128]{3,2,1,0:T(8,128)(2,1)}, u32[]{:S(2)}, u32[]{:S(2)}) collective-permute-start(bf16[8,32,64,128]{3,2,1,0:T(8,128)(2,1)} %shard_map.50.refs_0_), channel_id=1, source_target_pairs={{0,1},{1,0},{2,3},{3,2},{4,5},{5,4},{6,7},{7,6},{8,9},{9,8},{10,11... | collective-permute-start | bytes 12582920 | tf_op jit(solution)/shard_map/ppermute | solution.py:16
  411.0 123.8 %collective-permute-start.14 = (bf16[8,32,64,128]{3,2,1,0:T(8,128)(2,1)}, bf16[8,32,64,128]{3,2,1,0:T(8,128)(2,1)}, u32[]{:S(2)}, u32[]{:S(2)}) collective-permute-start(bf16[8,32,64,128]{3,2,1,0:T(8,128)(2,1)} %shard_map.47.refs_0_), channel_id=1, source_target_pairs={{0,1},{1,0},{2,3},{3,2},{4,5},{5,4},{6,7},{7,6},{8,9},{9,8},{10,11... | collective-permute-start | bytes 12582920 | tf_op jit(solution)/shard_map/ppermute | solution.py:16
  412.7 71.4 %collective-permute-start.15 = (bf16[1,32,128,128]{3,2,1,0:T(8,128)(2,1)S(1)}, bf16[1,32,128,128]{3,2,1,0:T(8,128)(2,1)S(1)}, u32[]{:S(2)}, u32[]{:S(2)}) collective-permute-start(bf16[1,32,128,128]{3,2,1,0:T(8,128)(2,1)S(1)} %get-tuple-element.54), channel_id=1, source_target_pairs={{0,8},{1,9},{2,10},{3,11},{4,12},{5,13},{6,14},{7,15},{8,0},{9,1},... | collective-permute-start | bytes 3145736 | tf_op jit(solution)/shard_map/ppermute | solution.py:16
  416.0 90.6 %collective-permute-start.17 = (bf16[1,32,128,128]{3,2,1,0:T(8,128)(2,1)S(1)}, bf16[1,32,128,128]{3,2,1,0:T(8,128)(2,1)S(1)}, u32[]{:S(2)}, u32[]{:S(2)}) collective-permute-start(bf16[1,32,128,128]{3,2,1,0:T(8,128)(2,1)S(1)} %get-tuple-element.53), channel_id=1, source_target_pairs={{0,8},{1,9},{2,10},{3,11},{4,12},{5,13},{6,14},{7,15},{8,0},{9,1},... | collective-permute-start | bytes 3145736 | tf_op jit(solution)/shard_map/ppermute | solution.py:16
  484.1 38.1 %collective-permute-start.16 = (bf16[1,32,128,128]{3,2,1,0:T(8,128)(2,1)S(1)}, bf16[1,32,128,128]{3,2,1,0:T(8,128)(2,1)S(1)}, u32[]{:S(2)}, u32[]{:S(2)}) collective-permute-start(bf16[1,32,128,128]{3,2,1,0:T(8,128)(2,1)S(1)} %collective-permute-done.15), channel_id=1, source_target_pairs={{0,16},{16,0},{1,17},{17,1},{2,18},{18,2},{3,19},{19,3},{4,20},{20... | collective-permute-start | bytes 3145736 | tf_op jit(solution)/shard_map/ppermute | solution.py:16
  506.6 23.9 %collective-permute-start.18 = (bf16[1,32,128,128]{3,2,1,0:T(8,128)(2,1)S(1)}, bf16[1,32,128,128]{3,2,1,0:T(8,128)(2,1)}, u32[]{:S(2)}, u32[]{:S(2)}) collective-permute-start(bf16[1,32,128,128]{3,2,1,0:T(8,128)(2,1)S(1)} %collective-permute-done.17), channel_id=1, source_target_pairs={{0,16},{16,0},{1,17},{17,1},{2,18},{18,2},{3,19},{19,3},{4,20},{20... | collective-permute-start | bytes 3145736 | tf_op jit(solution)/shard_map/ppermute | solution.py:16
  519.8 31.7 %collective-permute-start.28 = (bf16[32,64,128]{2,1,0:T(8,128)(2,1)}, bf16[32,64,128]{2,1,0:T(8,128)(2,1)}, u32[]{:S(2)}, u32[]{:S(2)}) collective-permute-start(bf16[32,64,128]{2,1,0:T(8,128)(2,1)} %get-tuple-element.46), channel_id=1, source_target_pairs={{0,1},{1,0},{2,3},{3,2},{4,5},{5,4},{6,7},{7,6},{8,9},{9,8},{10,11... | collective-permute-start | bytes 1572872 | tf_op jit(solution)/shard_map/ppermute | solution.py:16
  520.9 31.4 %collective-permute-start.29 = (bf16[32,64,128]{2,1,0:T(8,128)(2,1)}, bf16[32,64,128]{2,1,0:T(8,128)(2,1)}, u32[]{:S(2)}, u32[]{:S(2)}) collective-permute-start(bf16[32,64,128]{2,1,0:T(8,128)(2,1)} %get-tuple-element.47), channel_id=1, source_target_pairs={{0,2},{1,3},{2,0},{3,1},{4,6},{5,7},{6,4},{7,5},{8,10},{9,11},{10,... | collective-permute-start | bytes 1572872 | tf_op jit(solution)/shard_map/ppermute | solution.py:16
  522.2 30.6 %collective-permute-start.30 = (bf16[32,64,128]{2,1,0:T(8,128)(2,1)}, bf16[32,64,128]{2,1,0:T(8,128)(2,1)}, u32[]{:S(2)}, u32[]{:S(2)}) collective-permute-start(bf16[32,64,128]{2,1,0:T(8,128)(2,1)} %get-tuple-element.48), channel_id=1, source_target_pairs={{0,3},{1,2},{2,1},{3,0},{4,7},{5,6},{6,5},{7,4},{8,11},{9,10},{10,... | collective-permute-start | bytes 1572872 | tf_op jit(solution)/shard_map/ppermute | solution.py:16
  530.4 23.9 %collective-permute-start.31 = (bf16[32,64,128]{2,1,0:T(8,128)(2,1)}, bf16[32,64,128]{2,1,0:T(8,128)(2,1)}, u32[]{:S(2)}, u32[]{:S(2)}) collective-permute-start(bf16[32,64,128]{2,1,0:T(8,128)(2,1)} %get-tuple-element.49), channel_id=1, source_target_pairs={{0,4},{1,5},{2,6},{3,7},{4,0},{5,1},{6,2},{7,3},{8,12},{9,13},{10,... | collective-permute-start | bytes 1572872 | tf_op jit(solution)/shard_map/ppermute | solution.py:16
  534.8 21.0 %collective-permute-start.32 = (bf16[32,64,128]{2,1,0:T(8,128)(2,1)}, bf16[32,64,128]{2,1,0:T(8,128)(2,1)S(1)}, u32[]{:S(2)}, u32[]{:S(2)}) collective-permute-start(bf16[32,64,128]{2,1,0:T(8,128)(2,1)} %get-tuple-element.50), channel_id=1, source_target_pairs={{0,5},{1,4},{2,7},{3,6},{4,1},{5,0},{6,3},{7,2},{8,13},{9,12},{10,... | collective-permute-start | bytes 1572872 | tf_op jit(solution)/shard_map/ppermute | solution.py:16
  552.4 29.0 %collective-permute-start.34 = (bf16[32,64,128]{2,1,0:T(8,128)(2,1)}, bf16[32,64,128]{2,1,0:T(8,128)(2,1)S(1)}, u32[]{:S(2)}, u32[]{:S(2)}) collective-permute-start(bf16[32,64,128]{2,1,0:T(8,128)(2,1)} %get-tuple-element.52), channel_id=1, source_target_pairs={{0,7},{1,6},{2,5},{3,4},{4,3},{5,2},{6,1},{7,0},{8,15},{9,14},{10,... | collective-permute-start | bytes 1572872 | tf_op jit(solution)/shard_map/ppermute | solution.py:16
  552.8 28.5 %collective-permute-start.19 = (bf16[32,64,128]{2,1,0:T(8,128)(2,1)}, bf16[32,64,128]{2,1,0:T(8,128)(2,1)S(1)}, u32[]{:S(2)}, u32[]{:S(2)}) collective-permute-start(bf16[32,64,128]{2,1,0:T(8,128)(2,1)} %get-tuple-element.38), channel_id=1, source_target_pairs={{0,1},{1,0},{2,3},{3,2},{4,5},{5,4},{6,7},{7,6},{8,9},{9,8},{10,11... | collective-permute-start | bytes 1572872 | tf_op jit(solution)/shard_map/ppermute | solution.py:16
  554.3 35.7 %collective-permute-start.20 = (bf16[32,64,128]{2,1,0:T(8,128)(2,1)}, bf16[32,64,128]{2,1,0:T(8,128)(2,1)S(1)}, u32[]{:S(2)}, u32[]{:S(2)}) collective-permute-start(bf16[32,64,128]{2,1,0:T(8,128)(2,1)} %get-tuple-element.39), channel_id=1, source_target_pairs={{0,2},{1,3},{2,0},{3,1},{4,6},{5,7},{6,4},{7,5},{8,10},{9,11},{10,... | collective-permute-start | bytes 1572872 | tf_op jit(solution)/shard_map/ppermute | solution.py:16
  555.8 46.1 %collective-permute-start.21 = (bf16[32,64,128]{2,1,0:T(8,128)(2,1)}, bf16[32,64,128]{2,1,0:T(8,128)(2,1)S(1)}, u32[]{:S(2)}, u32[]{:S(2)}) collective-permute-start(bf16[32,64,128]{2,1,0:T(8,128)(2,1)} %get-tuple-element.40), channel_id=1, source_target_pairs={{0,3},{1,2},{2,1},{3,0},{4,7},{5,6},{6,5},{7,4},{8,11},{9,10},{10,... | collective-permute-start | bytes 1572872 | tf_op jit(solution)/shard_map/ppermute | solution.py:16
  567.0 34.9 %collective-permute-start.22 = (bf16[32,64,128]{2,1,0:T(8,128)(2,1)}, bf16[32,64,128]{2,1,0:T(8,128)(2,1)}, u32[]{:S(2)}, u32[]{:S(2)}) collective-permute-start(bf16[32,64,128]{2,1,0:T(8,128)(2,1)} %get-tuple-element.41), channel_id=1, source_target_pairs={{0,4},{1,5},{2,6},{3,7},{4,0},{5,1},{6,2},{7,3},{8,12},{9,13},{10,... | collective-permute-start | bytes 1572872 | tf_op jit(solution)/shard_map/ppermute | solution.py:16
  581.4 20.5 %collective-permute-start.23 = (bf16[32,64,128]{2,1,0:T(8,128)(2,1)}, bf16[32,64,128]{2,1,0:T(8,128)(2,1)}, u32[]{:S(2)}, u32[]{:S(2)}) collective-permute-start(bf16[32,64,128]{2,1,0:T(8,128)(2,1)} %get-tuple-element.42), channel_id=1, source_target_pairs={{0,5},{1,4},{2,7},{3,6},{4,1},{5,0},{6,3},{7,2},{8,13},{9,12},{10,... | collective-permute-start | bytes 1572872 | tf_op jit(solution)/shard_map/ppermute | solution.py:16
  581.4 30.6 %collective-permute-start.24 = (bf16[32,64,128]{2,1,0:T(8,128)(2,1)}, bf16[32,64,128]{2,1,0:T(8,128)(2,1)}, u32[]{:S(2)}, u32[]{:S(2)}) collective-permute-start(bf16[32,64,128]{2,1,0:T(8,128)(2,1)} %get-tuple-element.43), channel_id=1, source_target_pairs={{0,6},{1,7},{2,4},{3,5},{4,2},{5,3},{6,0},{7,1},{8,14},{9,15},{10,... | collective-permute-start | bytes 1572872 | tf_op jit(solution)/shard_map/ppermute | solution.py:16
  590.0 34.7 %collective-permute-start.25 = (bf16[32,64,128]{2,1,0:T(8,128)(2,1)}, bf16[32,64,128]{2,1,0:T(8,128)(2,1)}, u32[]{:S(2)}, u32[]{:S(2)}) collective-permute-start(bf16[32,64,128]{2,1,0:T(8,128)(2,1)} %get-tuple-element.44), channel_id=1, source_target_pairs={{0,7},{1,6},{2,5},{3,4},{4,3},{5,2},{6,1},{7,0},{8,15},{9,14},{10,... | collective-permute-start | bytes 1572872 | tf_op jit(solution)/shard_map/ppermute | solution.py:16
  (16 other events, 681.2 us)
where the time goes:
time: 630 us; the launch traced here: 629 us
  waiting for transfers between devices  475 us (75%)
  Pallas kernels  95.4 us (15%)
  starting transfers between devices  37.1 us (6%)
  other arithmetic  13.4 us (2%)
  local copies, waits for them, and re-layouts  8.4 us (1%)
    ppermute x35, waiting for transfers between devices, swap(): return lax.ppermute(block, axis, [(i, i ^ offset) for i in range(count)])  475 us
    pallas_call x6, Pallas kernels, two_layers(): pl.pallas_call(functools.partial(layers_kernel, plan), out_shape=out_shap...  79.4 us
    ppermute x35, starting transfers between devices, swap(): return lax.ppermute(block, axis, [(i, i ^ offset) for i in range(count)])  37.1 us
    concatenate x4, other arithmetic, local(): joined = jnp.concatenate(held, axis=1)  12.8 us
  transfers between devices with their start and end apart: 35, of which 20 were waited for; matrix products, arithmetic and copies ran while one was open for 3% of the time, Pallas kernels for 14%

commit v1 on v0

--- a/solution.py
+++ b/solution.py
@@ -132,7 +132,7 @@
 
 
 def layers_kernel(plan, cols_ref, me_ref, *refs):
-    sources, half, flip, joined_out, step, layer, blocks = plan
+    sources, half, flip, joined_out, step, layer, blocks, paired = plan
     refs = list(refs)
     src = [refs.pop(0) for _ in range(sources)]
     other = refs.pop(0) if sources == 1 else None
@@ -142,6 +142,7 @@
     outs = refs
     phase, at = pl.program_id(0), pl.program_id(1)
     count, _, rows, _ = middle.shape
+    swapped = me_ref[1] == 1
 
     def whole(ref, k):
         return ref[:, k].reshape(count * rows, 128)
@@ -162,11 +163,17 @@
     def run(p, own_of, partner_of, store):
         for t in range(step):
             k = at * step + t
-            c = cols_ref[((layer + p) * 2 + half) * blocks + k]
+            c = cols_ref[(layer + p) * blocks + k]
             both = jnp.concatenate([own_of(k), partner_of(c)], axis=1)
-            taken = jnp.concatenate([w[p][0][0, t], w[p][1][0, t]], axis=0)
+            first, second = w[p][0][0, t], w[p][1][0, t]
+            if paired:
+                first, second = (
+                    jnp.where(swapped, second, first),
+                    jnp.where(swapped, first, second),
+                )
+            taken = jnp.concatenate([first, second], axis=0)
             summed = jnp.dot(both, taken, preferred_element_type=jnp.float32)
-            summed = summed + bias[0, 0, t]
+            summed = summed + bias[0, t]
             store(k, t, jnp.clip(summed, 0.0, ceiling).astype(jnp.bfloat16))
 
     @pl.when(phase == 0)
@@ -191,14 +198,17 @@
 def two_layers(
     cols, me, source, other, weights, far, biases, layer, half, rows, count, flip, joined_out
 ):
-    blocks = biases.shape[2]
+    blocks = biases.shape[1]
     part = weights.shape[2]
+    paired = half == 1 and len(far[0][0]) == 2
     step = min(8, part, blocks)
     steps = blocks // step
 
     def weight_spec(p, which):
         def index(phase, at, cols, me):
             at = jnp.where(phase == p, at, (steps - 1) if p == 0 else 0)
+            if paired:
+                return (far[p][1], at, 0, 0)
             first = which * blocks + at * step
             piece, row = first // part, (first % part) // step
             if half == 0:
@@ -217,8 +227,8 @@
     for p in range(2):
         for which in range(2):
             specs.append(weight_spec(p, which))
-            operands.append(own if half == 0 else far[p][0])
-    specs.append(pl.BlockSpec((1, 1, step, 1, 128), lambda p, a, c, m: (layer + p, half, a, 0, 0)))
+            operands.append(own if half == 0 else far[p][0][which if paired else 0])
+    specs.append(pl.BlockSpec((1, step, 1, 128), lambda p, a, c, m: (layer + p, a, 0, 0)))
     operands.append(biases)
     if joined_out:
         out_shape = jax.ShapeDtypeStruct((count, blocks, rows, 128), jnp.bfloat16)
@@ -226,7 +236,7 @@
     else:
         out_shape = [jax.ShapeDtypeStruct((blocks, rows, 128), jnp.bfloat16)] * count
         out_specs = [pl.BlockSpec((step, rows, 128), lambda p, a, c, m: (a * p, 0, 0))] * count
-    plan = (1 if other is not None else count, half, flip, joined_out, step, layer, blocks)
+    plan = (1 if other is not None else count, half, flip, joined_out, step, layer, blocks, paired)
     cells = count * rows * blocks
     return pl.pallas_call(
         functools.partial(layers_kernel, plan),
@@ -247,7 +257,7 @@
 
 
 def far_batches(layer_count):
-    return [(l, 2) for l in range(0, layer_count - 2, 2)] + [
+    return [(0, 1), (1, 1)] + [(l, 2) for l in range(2, layer_count - 2, 2)] + [
         (layer_count - 2, 1),
         (layer_count - 1, 1),
     ]
@@ -269,15 +279,15 @@
     slab, group = lax.axis_index("slab"), lax.axis_index("groups")
     me = jnp.stack([slab, group]).astype(jnp.int32)
 
+    far_bias = swap(biases, "slab", 1 << first_bit)
+    far_columns = swap(columns, "slab", 1 << first_bit)
+    bias = [one.reshape(layer_count, blocks, 1, width) for one in (biases, far_bias)]
+    cols = [one.reshape(-1) for one in (columns, far_columns)]
+
     mine = split(me, activations, offsets, first_bit, blocks)
     pieces = [mine[0]]
     for j in range(1, count):
         pieces.append(swap(mine[j], "slab", offsets[j]))
-
-    far_bias = swap(biases, "slab", 1 << first_bit)
-    far_columns = swap(columns, "slab", 1 << first_bit)
-    bias = jnp.stack([biases, far_bias], axis=1).reshape(layer_count, 2, blocks, 1, width)
-    cols = jnp.stack([columns, far_columns], axis=1).reshape(-1)
 
     part = 2 * blocks // group_count
     parts = weights.reshape(layer_count, group_count, part, width, width)
@@ -292,8 +302,9 @@
             for one in held:
                 got.append(swap(one, "groups", 1 << b))
             held = held + got
-        joined = jnp.concatenate(held, axis=1)
-        far += [(joined, i) for i in range(size)]
+        if group_count != 2:
+            held = [jnp.concatenate(held, axis=1)]
+        far += [(held, i) for i in range(size)]
 
     def weights_of(half, layer):
         return [None, None] if half == 0 else far[layer : layer + 2]
@@ -307,7 +318,7 @@
                 other = swap(halves[half], "slab", 1 << bits[m])
                 flip = offsets.index(1 << bits[m])
             halves[half] = two_layers(
-                cols, me, halves[half], other, parts, weights_of(half, 2 * m), bias,
+                cols[half], me, halves[half], other, parts, weights_of(half, 2 * m), bias[half],
                 2 * m, half, rows, count, flip, not last,
             )
     output = None

time: 630 us -> 574 us (0.911)
  waiting for transfers between devices: 475 us -> 423 us
  other arithmetic: 13.4 us -> 0.56 us
  starting transfers between devices: 37.1 us -> 44.7 us
    ppermute x35 -> x37, waiting for transfers between devices: 475 us -> 423 us  [swap(): return lax.ppermute(block, axis, [(i, i ^ offset) for i in range(count)])]
    concatenate x4 -> x0, other arithmetic: 12.8 us -> none  [local(): joined = jnp.concatenate(held, axis=1)]
    ppermute x35 -> x37, starting transfers between devices: 37.1 us -> 44.7 us  [swap(): return lax.ppermute(block, axis, [(i, i ^ offset) for i in range(count)])]
  transfers between devices with their start and end apart: 35 -> 37, of which waited for: 20 -> 21; matrix products, arithmetic and copies ran while one was open for 3% -> 2% of each run, Pallas kernels for 14% -> 14%
where the time goes in v1:
time: 574 us; the launch traced here: 573 us
  waiting for transfers between devices  423 us (74%)
  Pallas kernels  94.4 us (16%)
  starting transfers between devices  44.7 us (8%)
  local copies, waits for them, and re-layouts  10.2 us (2%)
    ppermute x37, waiting for transfers between devices, swap(): return lax.ppermute(block, axis, [(i, i ^ offset) for i in range(count)])  423 us
    pallas_call x6, Pallas kernels, two_layers(): pl.pallas_call(functools.partial(layers_kernel, plan), out_shape=out_shap...  78.7 us
    ppermute x37, starting transfers between devices, swap(): return lax.ppermute(block, axis, [(i, i ^ offset) for i in range(count)])  44.7 us
  transfers between devices with their start and end apart: 37, of which 21 were waited for; matrix products, arithmetic and copies ran while one was open for 2% of the time, Pallas kernels for 14%

profile of v1, /device:TPU:1, one launch (start us, length us, event | category | flops | bytes accessed | tf_op | source)
XLA Modules:
  0.0 573.3 jit_solution(17923667456498006795)
XLA Ops:
  0.6 7.0 %split.1 = (bf16[2,32,64,128]{3,2,1,0:T(8,128)(2,1)}, bf16[2,32,64,128]{3,2,1,0:T(8,128)(2,1)}, bf16[2,32,64,128]{3,2,1,0:T(8,128)(2,1)}, bf16[2,32,64,128]{3,2,...) custom-call(s32[2]{0:T(128)} %pad_add_fusion.me_ref, ...), custom_call_target="tpu_custom_call" | custom-call | bytes 16777216 | tf_op jit(solution)/shard_map/split/pallas_call | solution.py:55
  12.1 4.1 dynamic-slice_bitcast_fusion.1
  18.6 15.5 %collective-permute-done.2.refs_2_ = bf16[2,32,64,128]{3,2,1,0:T(8,128)(2,1)S(1)} collective-permute-done((bf16[2,32,64,128]{3,2,1,0:T(8,128)(2,1)}, bf16[2,32,64,128]{3,2,1,0:T(8,128)(2,1)S(1)}, u32[]{:S(2)}, u32[]{:S(2)}) %collective-permute-start.2) | collective-permute-done | bytes 1048608 | tf_op jit(solution)/shard_map/ppermute | solution.py:16
  36.6 20.2 %collective-permute-done.3.refs_3_ = bf16[2,32,64,128]{3,2,1,0:T(8,128)(2,1)S(1)} collective-permute-done((bf16[2,32,64,128]{3,2,1,0:T(8,128)(2,1)}, bf16[2,32,64,128]{3,2,1,0:T(8,128)(2,1)S(1)}, u32[]{:S(2)}, u32[]{:S(2)}) %collective-permute-start.3) | collective-permute-done | bytes 1048608 | tf_op jit(solution)/shard_map/ppermute | solution.py:16
  59.4 27.1 %collective-permute-done.8.refs_8_ = bf16[1,32,128,128]{3,2,1,0:T(8,128)(2,1)} collective-permute-done((bf16[1,32,128,128]{3,2,1,0:T(8,128)(2,1)S(1)}, bf16[1,32,128,128]{3,2,1,0:T(8,128)(2,1)}, u32[]{:S(2)}, u32[]{:S(2)}) %collective-permute-start.8) | collective-permute-done | bytes 1048608 | tf_op jit(solution)/shard_map/ppermute | solution.py:16
  87.8 21.3 %collective-permute-done.10.refs_10_ = bf16[1,32,128,128]{3,2,1,0:T(8,128)(2,1)} collective-permute-done((bf16[1,32,128,128]{3,2,1,0:T(8,128)(2,1)S(1)}, bf16[1,32,128,128]{3,2,1,0:T(8,128)(2,1)}, u32[]{:S(2)}, u32[]{:S(2)}) %collective-permute-start.10) | collective-permute-done | bytes 1048608 | tf_op jit(solution)/shard_map/ppermute | solution.py:16
  111.7 14.9 %collective-permute-done.6.refs_6_ = bf16[2,32,64,128]{3,2,1,0:T(8,128)(2,1)} collective-permute-done((bf16[2,32,64,128]{3,2,1,0:T(8,128)(2,1)}, bf16[2,32,64,128]{3,2,1,0:T(8,128)(2,1)}, u32[]{:S(2)}, u32[]{:S(2)}) %collective-permute-start.6) | collective-permute-done | bytes 1048608 | tf_op jit(solution)/shard_map/ppermute | solution.py:16
  126.5 22.8 %collective-permute-done.7.refs_7_ = bf16[2,32,64,128]{3,2,1,0:T(8,128)(2,1)} collective-permute-done((bf16[2,32,64,128]{3,2,1,0:T(8,128)(2,1)}, bf16[2,32,64,128]{3,2,1,0:T(8,128)(2,1)}, u32[]{:S(2)}, u32[]{:S(2)}) %collective-permute-start.7) | collective-permute-done | bytes 1048608 | tf_op jit(solution)/shard_map/ppermute | solution.py:16
  149.3 13.2 %shard_map.49.refs_0_ = bf16[8,32,64,128]{3,2,1,0:T(8,128)(2,1)} custom-call(s32[192]{0:T(256)} %reshape.39.cols_ref, s32[2]{0:T(128)} %pad_add_fusion.me_ref, bf16[2,32,64,128]{3,2,1,0:T(8,128)(2,1)} %get-tuple-element.29.refs_0_, bf16[2,32,64,128]{3,2,1,0:T(8,128)(2,1)} %copy-done.1, bf16[2,32,64,128]{3,2,1,0:T(8,128)(2,1)} %copy-done.2, ...), custom_call_target="tpu_custom_call" | custom-call | flops 2147483648 | bytes 16777216 | tf_op jit(solution)/shard_map/pallas_call | solution.py:241
  165.2 3.2 dynamic-slice_bitcast_fusion
  171.3 46.9 %collective-permute-done.12 = f32[6,4096]{1,0:T(8,128)S(1)} collective-permute-done((f32[6,4096]{1,0:T(8,128)S(1)}, f32[6,4096]{1,0:T(8,128)S(1)}, u32[]{:S(2)}, u32[]{:S(2)}) %collective-permute-start.12) | collective-permute-done | bytes 98336 | tf_op jit(solution)/shard_map/ppermute | solution.py:16
  219.0 12.9 %shard_map.46.refs_0_ = bf16[8,32,64,128]{3,2,1,0:T(8,128)(2,1)} custom-call(s32[192]{0:T(256)} %reshape.32.cols_ref, s32[2]{0:T(128)} %pad_add_fusion.me_ref, bf16[2,32,64,128]{3,2,1,0:T(8,128)(2,1)} %get-tuple-element.29.refs_0_, bf16[2,32,64,128]{3,2,1,0:T(8,128)(2,1)} %copy-done.1, bf16[2,32,64,128]{3,2,1,0:T(8,128)(2,1)} %copy-done.2, ...), custom_call_target="tpu_custom_call" | custom-call | flops 2147483648 | bytes 16777216 | tf_op jit(solution)/shard_map/pallas_call | solution.py:241
  233.2 30.0 %collective-permute-done.14.refs_2_.refs_4_ = bf16[2,32,128,128]{3,2,1,0:T(8,128)(2,1)S(1)} collective-permute-done((bf16[2,32,128,128]{3,2,1,0:T(8,128)(2,1)}, bf16[2,32,128,128]{3,2,1,0:T(8,128)(2,1)S(1)}, u32[]{:S(2)}, u32[]{:S(2)}) %collective-permute-start.14) | collective-permute-done | bytes 2097184 | tf_op jit(solution)/shard_map/ppermute | solution.py:16
  264.4 13.1 %shard_map.50.refs_0_ = bf16[8,32,64,128]{3,2,1,0:T(8,128)(2,1)} custom-call(s32[192]{0:T(256)} %reshape.39.cols_ref, s32[2]{0:T(128)} %pad_add_fusion.me_ref, bf16[8,32,64,128]{3,2,1,0:T(8,128)(2,1)} %shard_map.49.refs_0_, bf16[8,32,64,128]{3,2,1,0:T(8,128)(2,1)} %collective-permute-done.28.refs_1_, bf16[6,64,128,128]{3,2,1,0:T(8,128)(2,1)} %bitcast.17, ...), custom_call_target="tpu_custom_call" | custom-call | flops 2147483648 | bytes 16777216 | tf_op jit(solution)/shard_map/pallas_call | solution.py:241
  279.3 29.7 %collective-permute-done.15.refs_3_.refs_5_ = bf16[2,32,128,128]{3,2,1,0:T(8,128)(2,1)} collective-permute-done((bf16[2,32,128,128]{3,2,1,0:T(8,128)(2,1)S(1)}, bf16[2,32,128,128]{3,2,1,0:T(8,128)(2,1)}, u32[]{:S(2)}, u32[]{:S(2)}) %collective-permute-start.15) | collective-permute-done | bytes 2097184 | tf_op jit(solution)/shard_map/ppermute | solution.py:16
  309.0 35.8 %collective-permute-done.13.refs_1_ = bf16[8,32,64,128]{3,2,1,0:T(8,128)(2,1)} collective-permute-done((bf16[8,32,64,128]{3,2,1,0:T(8,128)(2,1)}, bf16[8,32,64,128]{3,2,1,0:T(8,128)(2,1)}, u32[]{:S(2)}, u32[]{:S(2)}) %collective-permute-start.13) | collective-permute-done | bytes 4194336 | tf_op jit(solution)/shard_map/ppermute | solution.py:16
  344.8 13.0 %shard_map.47.refs_0_ = bf16[8,32,64,128]{3,2,1,0:T(8,128)(2,1)} custom-call(s32[192]{0:T(256)} %reshape.32.cols_ref, s32[2]{0:T(128)} %pad_add_fusion.me_ref, bf16[8,32,64,128]{3,2,1,0:T(8,128)(2,1)} %shard_map.46.refs_0_, bf16[8,32,64,128]{3,2,1,0:T(8,128)(2,1)} %collective-permute-done.13.refs_1_, bf16[2,32,128,128]{3,2,1,0:T(8,128)(2,1)} %copy-done, ...), custom_call_target="tpu_custom_call" | custom-call | flops 2147483648 | bytes 16777216 | tf_op jit(solution)/shard_map/pallas_call | solution.py:241
  361.1 68.3 %collective-permute-done.17.refs_2_ = bf16[1,32,128,128]{3,2,1,0:T(8,128)(2,1)S(1)} collective-permute-done((bf16[1,32,128,128]{3,2,1,0:T(8,128)(2,1)}, bf16[1,32,128,128]{3,2,1,0:T(8,128)(2,1)S(1)}, u32[]{:S(2)}, u32[]{:S(2)}) %collective-permute-start.17) | collective-permute-done | bytes 1048608 | tf_op jit(solution)/shard_map/ppermute | solution.py:16
  430.7 21.3 %collective-permute-done.19.refs_4_ = bf16[1,32,128,128]{3,2,1,0:T(8,128)(2,1)S(1)} collective-permute-done((bf16[1,32,128,128]{3,2,1,0:T(8,128)(2,1)S(1)}, bf16[1,32,128,128]{3,2,1,0:T(8,128)(2,1)S(1)}, u32[]{:S(2)}, u32[]{:S(2)}) %collective-permute-start.19) | collective-permute-done | bytes 1048608 | tf_op jit(solution)/shard_map/ppermute | solution.py:16
  453.1 13.2 %shard_map.51 = (bf16[32,64,128]{2,1,0:T(8,128)(2,1)}, bf16[32,64,128]{2,1,0:T(8,128)(2,1)}, bf16[32,64,128]{2,1,0:T(8,128)(2,1)}, bf16[32,64,128]{2,1,0:T(8,128...) custom-call(s32[192]{0:T(256)} %reshape.39.cols_ref, ...), custom_call_target="tpu_custom_call" | custom-call | flops 2147483648 | bytes 16777216 | tf_op jit(solution)/shard_map/pallas_call | solution.py:241
  469.3 6.5 %collective-permute-done.20.refs_5_ = bf16[1,32,128,128]{3,2,1,0:T(8,128)(2,1)S(1)} collective-permute-done((bf16[1,32,128,128]{3,2,1,0:T(8,128)(2,1)S(1)}, bf16[1,32,128,128]{3,2,1,0:T(8,128)(2,1)S(1)}, u32[]{:S(2)}, u32[]{:S(2)}) %collective-permute-start.20) | collective-permute-done | bytes 1048608 | tf_op jit(solution)/shard_map/ppermute | solution.py:16
  479.1 13.2 %shard_map.48 = (bf16[32,64,128]{2,1,0:T(8,128)(2,1)}, bf16[32,64,128]{2,1,0:T(8,128)(2,1)}, bf16[32,64,128]{2,1,0:T(8,128)(2,1)}, bf16[32,64,128]{2,1,0:T(8,128...) custom-call(s32[192]{0:T(256)} %reshape.32.cols_ref, ...), custom_call_target="tpu_custom_call" | custom-call | flops 2147483648 | bytes 16777216 | tf_op jit(solution)/shard_map/pallas_call | solution.py:241
  495.6 7.8 %collective-permute-done.34.refs_5_ = bf16[32,64,128]{2,1,0:T(8,128)(2,1)S(1)} collective-permute-done((bf16[32,64,128]{2,1,0:T(8,128)(2,1)}, bf16[32,64,128]{2,1,0:T(8,128)(2,1)S(1)}, u32[]{:S(2)}, u32[]{:S(2)}) %collective-permute-start.34) | collective-permute-done | bytes 524320 | tf_op jit(solution)/shard_map/ppermute | solution.py:16
  503.4 7.4 %collective-permute-done.35.refs_6_ = bf16[32,64,128]{2,1,0:T(8,128)(2,1)S(1)} collective-permute-done((bf16[32,64,128]{2,1,0:T(8,128)(2,1)}, bf16[32,64,128]{2,1,0:T(8,128)(2,1)S(1)}, u32[]{:S(2)}, u32[]{:S(2)}) %collective-permute-start.35) | collective-permute-done | bytes 524320 | tf_op jit(solution)/shard_map/ppermute | solution.py:16
  512.5 13.2 %collective-permute-done.36.refs_7_ = bf16[32,64,128]{2,1,0:T(8,128)(2,1)S(1)} collective-permute-done((bf16[32,64,128]{2,1,0:T(8,128)(2,1)}, bf16[32,64,128]{2,1,0:T(8,128)(2,1)S(1)}, u32[]{:S(2)}, u32[]{:S(2)}) %collective-permute-start.36) | collective-permute-done | bytes 524320 | tf_op jit(solution)/shard_map/ppermute | solution.py:16
  527.6 3.8 collective-permute-done.22.refs_2_
  533.6 4.4 shard_map.52.refs_8_
  538.1 5.1 collective-permute-done.23.refs_3_
  543.2 5.0 collective-permute-done.25.refs_5_
  548.2 7.7 %collective-permute-done.26.refs_6_ = bf16[32,64,128]{2,1,0:T(8,128)(2,1)} collective-permute-done((bf16[32,64,128]{2,1,0:T(8,128)(2,1)}, bf16[32,64,128]{2,1,0:T(8,128)(2,1)}, u32[]{:S(2)}, u32[]{:S(2)}) %collective-permute-start.26) | collective-permute-done | bytes 524320 | tf_op jit(solution)/shard_map/ppermute | solution.py:16
  555.8 12.9 %collective-permute-done.27.refs_7_ = bf16[32,64,128]{2,1,0:T(8,128)(2,1)} collective-permute-done((bf16[32,64,128]{2,1,0:T(8,128)(2,1)}, bf16[32,64,128]{2,1,0:T(8,128)(2,1)}, u32[]{:S(2)}, u32[]{:S(2)}) %collective-permute-start.27) | collective-permute-done | bytes 524320 | tf_op jit(solution)/shard_map/ppermute | solution.py:16
  568.7 4.4 shard_map.53
  (92 shorter events, 48.2 us)
Async XLA Ops:
  7.6 26.5 %collective-permute-start.2 = (bf16[2,32,64,128]{3,2,1,0:T(8,128)(2,1)}, bf16[2,32,64,128]{3,2,1,0:T(8,128)(2,1)S(1)}, u32[]{:S(2)}, u32[]{:S(2)}) collective-permute-start(bf16[2,32,64,128]{3,2,1,0:T(8,128)(2,1)} %get-tuple-element.31), channel_id=1, source_target_pairs={{0,2},{1,3},{2,0},{3,1},{4,6},{5,7},{6,4},{7,5},{8,10},{9,11},{10,... | collective-permute-start | bytes 3145736 | tf_op jit(solution)/shard_map/ppermute | solution.py:16
  10.3 46.5 %collective-permute-start.3 = (bf16[2,32,64,128]{3,2,1,0:T(8,128)(2,1)}, bf16[2,32,64,128]{3,2,1,0:T(8,128)(2,1)S(1)}, u32[]{:S(2)}, u32[]{:S(2)}) collective-permute-start(bf16[2,32,64,128]{3,2,1,0:T(8,128)(2,1)} %get-tuple-element.32), channel_id=1, source_target_pairs={{0,3},{1,2},{2,1},{3,0},{4,7},{5,6},{6,5},{7,4},{8,11},{9,10},{10,... | collective-permute-start | bytes 3145736 | tf_op jit(solution)/shard_map/ppermute | solution.py:16
  10.4 48.9 %collective-permute-start.4 = (bf16[2,32,64,128]{3,2,1,0:T(8,128)(2,1)}, bf16[2,32,64,128]{3,2,1,0:T(8,128)(2,1)}, u32[]{:S(2)}, u32[]{:S(2)}) collective-permute-start(bf16[2,32,64,128]{3,2,1,0:T(8,128)(2,1)} %get-tuple-element.33), channel_id=1, source_target_pairs={{0,4},{1,5},{2,6},{3,7},{4,0},{5,1},{6,2},{7,3},{8,12},{9,13},{10,... | collective-permute-start | bytes 3145736 | tf_op jit(solution)/shard_map/ppermute | solution.py:16
  16.2 70.3 %collective-permute-start.8 = (bf16[1,32,128,128]{3,2,1,0:T(8,128)(2,1)S(1)}, bf16[1,32,128,128]{3,2,1,0:T(8,128)(2,1)}, u32[]{:S(2)}, u32[]{:S(2)}) collective-permute-start(bf16[1,32,128,128]{3,2,1,0:T(8,128)(2,1)S(1)} %get-tuple-element.56), channel_id=1, source_target_pairs={{0,8},{1,9},{2,10},{3,11},{4,12},{5,13},{6,14},{7,15},{8,0},{9,1},... | collective-permute-start | bytes 3145736 | tf_op jit(solution)/shard_map/ppermute | solution.py:16
  18.5 90.5 %collective-permute-start.10 = (bf16[1,32,128,128]{3,2,1,0:T(8,128)(2,1)S(1)}, bf16[1,32,128,128]{3,2,1,0:T(8,128)(2,1)}, u32[]{:S(2)}, u32[]{:S(2)}) collective-permute-start(bf16[1,32,128,128]{3,2,1,0:T(8,128)(2,1)S(1)} %get-tuple-element.55), channel_id=1, source_target_pairs={{0,8},{1,9},{2,10},{3,11},{4,12},{5,13},{6,14},{7,15},{8,0},{9,1},... | collective-permute-start | bytes 3145736 | tf_op jit(solution)/shard_map/ppermute | solution.py:16
  34.1 77.6 %collective-permute-start.5 = (bf16[2,32,64,128]{3,2,1,0:T(8,128)(2,1)}, bf16[2,32,64,128]{3,2,1,0:T(8,128)(2,1)}, u32[]{:S(2)}, u32[]{:S(2)}) collective-permute-start(bf16[2,32,64,128]{3,2,1,0:T(8,128)(2,1)} %get-tuple-element.34), channel_id=1, source_target_pairs={{0,5},{1,4},{2,7},{3,6},{4,1},{5,0},{6,3},{7,2},{8,13},{9,12},{10,... | collective-permute-start | bytes 3145736 | tf_op jit(solution)/shard_map/ppermute | solution.py:16
  56.8 69.7 %collective-permute-start.6 = (bf16[2,32,64,128]{3,2,1,0:T(8,128)(2,1)}, bf16[2,32,64,128]{3,2,1,0:T(8,128)(2,1)}, u32[]{:S(2)}, u32[]{:S(2)}) collective-permute-start(bf16[2,32,64,128]{3,2,1,0:T(8,128)(2,1)} %get-tuple-element.35), channel_id=1, source_target_pairs={{0,6},{1,7},{2,4},{3,5},{4,2},{5,3},{6,0},{7,1},{8,14},{9,15},{10,... | collective-permute-start | bytes 3145736 | tf_op jit(solution)/shard_map/ppermute | solution.py:16
  59.3 90.0 %collective-permute-start.7 = (bf16[2,32,64,128]{3,2,1,0:T(8,128)(2,1)}, bf16[2,32,64,128]{3,2,1,0:T(8,128)(2,1)}, u32[]{:S(2)}, u32[]{:S(2)}) collective-permute-start(bf16[2,32,64,128]{3,2,1,0:T(8,128)(2,1)} %get-tuple-element.36), channel_id=1, source_target_pairs={{0,7},{1,6},{2,5},{3,4},{4,3},{5,2},{6,1},{7,0},{8,15},{9,14},{10,... | collective-permute-start | bytes 3145736 | tf_op jit(solution)/shard_map/ppermute | solution.py:16
  86.5 132.5 %collective-permute-start.9 = (bf16[1,32,128,128]{3,2,1,0:T(8,128)(2,1)}, bf16[1,32,128,128]{3,2,1,0:T(8,128)(2,1)}, u32[]{:S(2)}, u32[]{:S(2)}) collective-permute-start(bf16[1,32,128,128]{3,2,1,0:T(8,128)(2,1)} %collective-permute-done.8.refs_8_), channel_id=1, source_target_pairs={{0,16},{16,0},{1,17},{17,1},{2,18},{18,2},{3,19},{19,3},{4,20},{20... | collective-permute-start | bytes 3145736 | tf_op jit(solution)/shard_map/ppermute | solution.py:16
  109.0 110.0 %collective-permute-start.11 = (bf16[1,32,128,128]{3,2,1,0:T(8,128)(2,1)}, bf16[1,32,128,128]{3,2,1,0:T(8,128)(2,1)}, u32[]{:S(2)}, u32[]{:S(2)}) collective-permute-start(bf16[1,32,128,128]{3,2,1,0:T(8,128)(2,1)} %collective-permute-done.10.refs_10_), channel_id=1, source_target_pairs={{0,16},{16,0},{1,17},{17,1},{2,18},{18,2},{3,19},{19,3},{4,20},{20... | collective-permute-start | bytes 3145736 | tf_op jit(solution)/shard_map/ppermute | solution.py:16
  162.5 101.8 %collective-permute-start.28 = (bf16[8,32,64,128]{3,2,1,0:T(8,128)(2,1)}, bf16[8,32,64,128]{3,2,1,0:T(8,128)(2,1)}, u32[]{:S(2)}, u32[]{:S(2)}) collective-permute-start(bf16[8,32,64,128]{3,2,1,0:T(8,128)(2,1)} %shard_map.49.refs_0_), channel_id=1, source_target_pairs={{0,2},{1,3},{2,0},{3,1},{4,6},{5,7},{6,4},{7,5},{8,10},{9,11},{10,... | collective-permute-start | bytes 12582920 | tf_op jit(solution)/shard_map/ppermute | solution.py:16
  165.1 53.1 %collective-permute-start.12 = (f32[6,4096]{1,0:T(8,128)S(1)}, f32[6,4096]{1,0:T(8,128)S(1)}, u32[]{:S(2)}, u32[]{:S(2)}) collective-permute-start(f32[6,4096]{1,0:T(8,128)S(1)} %copy-done.15), channel_id=1, source_target_pairs={{0,8},{1,9},{2,10},{3,11},{4,12},{5,13},{6,14},{7,15},{8,0},{9,1},... | collective-permute-start | bytes 294920 | tf_op jit(solution)/shard_map/ppermute | solution.py:16
  168.3 94.9 %collective-permute-start.14 = (bf16[2,32,128,128]{3,2,1,0:T(8,128)(2,1)}, bf16[2,32,128,128]{3,2,1,0:T(8,128)(2,1)S(1)}, u32[]{:S(2)}, u32[]{:S(2)}) collective-permute-start(bf16[2,32,128,128]{3,2,1,0:T(8,128)(2,1)} %dynamic-slice_bitcast_fusion), channel_id=1, source_target_pairs={{0,8},{1,9},{2,10},{3,11},{4,12},{5,13},{6,14},{7,15},{8,0},{9,1},... | collective-permute-start | bytes 6291464 | tf_op jit(solution)/shard_map/ppermute | solution.py:16
  231.9 112.9 %collective-permute-start.13 = (bf16[8,32,64,128]{3,2,1,0:T(8,128)(2,1)}, bf16[8,32,64,128]{3,2,1,0:T(8,128)(2,1)}, u32[]{:S(2)}, u32[]{:S(2)}) collective-permute-start(bf16[8,32,64,128]{3,2,1,0:T(8,128)(2,1)} %shard_map.46.refs_0_), channel_id=1, source_target_pairs={{0,2},{1,3},{2,0},{3,1},{4,6},{5,7},{6,4},{7,5},{8,10},{9,11},{10,... | collective-permute-start | bytes 12582920 | tf_op jit(solution)/shard_map/ppermute | solution.py:16
  263.2 45.8 %collective-permute-start.15 = (bf16[2,32,128,128]{3,2,1,0:T(8,128)(2,1)S(1)}, bf16[2,32,128,128]{3,2,1,0:T(8,128)(2,1)}, u32[]{:S(2)}, u32[]{:S(2)}) collective-permute-start(bf16[2,32,128,128]{3,2,1,0:T(8,128)(2,1)S(1)} %collective-permute-done.14.refs_2_.refs_4_), channel_id=1, source_target_pairs={{0,16},{16,0},{1,17},{17,1},{2,18},{18,2},{3,19},{19,3},{4,20},{20... | collective-permute-start | bytes 6291464 | tf_op jit(solution)/shard_map/ppermute | solution.py:16
  277.5 175.6 %collective-permute-start.29 = (bf16[8,32,64,128]{3,2,1,0:T(8,128)(2,1)}, bf16[8,32,64,128]{3,2,1,0:T(8,128)(2,1)}, u32[]{:S(2)}, u32[]{:S(2)}) collective-permute-start(bf16[8,32,64,128]{3,2,1,0:T(8,128)(2,1)} %shard_map.50.refs_0_), channel_id=1, source_target_pairs={{0,1},{1,0},{2,3},{3,2},{4,5},{5,4},{6,7},{7,6},{8,9},{9,8},{10,11... | collective-permute-start | bytes 12582920 | tf_op jit(solution)/shard_map/ppermute | solution.py:16
  357.8 119.6 %collective-permute-start.16 = (bf16[8,32,64,128]{3,2,1,0:T(8,128)(2,1)}, bf16[8,32,64,128]{3,2,1,0:T(8,128)(2,1)}, u32[]{:S(2)}, u32[]{:S(2)}) collective-permute-start(bf16[8,32,64,128]{3,2,1,0:T(8,128)(2,1)} %shard_map.47.refs_0_), channel_id=1, source_target_pairs={{0,1},{1,0},{2,3},{3,2},{4,5},{5,4},{6,7},{7,6},{8,9},{9,8},{10,11... | collective-permute-start | bytes 12582920 | tf_op jit(solution)/shard_map/ppermute | solution.py:16
  358.8 70.7 %collective-permute-start.17 = (bf16[1,32,128,128]{3,2,1,0:T(8,128)(2,1)}, bf16[1,32,128,128]{3,2,1,0:T(8,128)(2,1)S(1)}, u32[]{:S(2)}, u32[]{:S(2)}) collective-permute-start(bf16[1,32,128,128]{3,2,1,0:T(8,128)(2,1)} %get-tuple-element.54), channel_id=1, source_target_pairs={{0,8},{1,9},{2,10},{3,11},{4,12},{5,13},{6,14},{7,15},{8,0},{9,1},... | collective-permute-start | bytes 3145736 | tf_op jit(solution)/shard_map/ppermute | solution.py:16
  361.1 90.8 %collective-permute-start.19 = (bf16[1,32,128,128]{3,2,1,0:T(8,128)(2,1)S(1)}, bf16[1,32,128,128]{3,2,1,0:T(8,128)(2,1)S(1)}, u32[]{:S(2)}, u32[]{:S(2)}) collective-permute-start(bf16[1,32,128,128]{3,2,1,0:T(8,128)(2,1)S(1)} %copy-done.4), channel_id=1, source_target_pairs={{0,8},{1,9},{2,10},{3,11},{4,12},{5,13},{6,14},{7,15},{8,0},{9,1},... | collective-permute-start | bytes 3145736 | tf_op jit(solution)/shard_map/ppermute | solution.py:16
  429.5 38.4 %collective-permute-start.18 = (bf16[1,32,128,128]{3,2,1,0:T(8,128)(2,1)S(1)}, bf16[1,32,128,128]{3,2,1,0:T(8,128)(2,1)}, u32[]{:S(2)}, u32[]{:S(2)}) collective-permute-start(bf16[1,32,128,128]{3,2,1,0:T(8,128)(2,1)S(1)} %collective-permute-done.17.refs_2_), channel_id=1, source_target_pairs={{0,16},{16,0},{1,17},{17,1},{2,18},{18,2},{3,19},{19,3},{4,20},{20... | collective-permute-start | bytes 3145736 | tf_op jit(solution)/shard_map/ppermute | solution.py:16
  451.9 23.9 %collective-permute-start.20 = (bf16[1,32,128,128]{3,2,1,0:T(8,128)(2,1)S(1)}, bf16[1,32,128,128]{3,2,1,0:T(8,128)(2,1)S(1)}, u32[]{:S(2)}, u32[]{:S(2)}) collective-permute-start(bf16[1,32,128,128]{3,2,1,0:T(8,128)(2,1)S(1)} %collective-permute-done.19.refs_4_), channel_id=1, source_target_pairs={{0,16},{16,0},{1,17},{17,1},{2,18},{18,2},{3,19},{19,3},{4,20},{20... | collective-permute-start | bytes 3145736 | tf_op jit(solution)/shard_map/ppermute | solution.py:16
  466.4 26.0 %collective-permute-start.30 = (bf16[32,64,128]{2,1,0:T(8,128)(2,1)}, bf16[32,64,128]{2,1,0:T(8,128)(2,1)}, u32[]{:S(2)}, u32[]{:S(2)}) collective-permute-start(bf16[32,64,128]{2,1,0:T(8,128)(2,1)} %get-tuple-element.46), channel_id=1, source_target_pairs={{0,1},{1,0},{2,3},{3,2},{4,5},{5,4},{6,7},{7,6},{8,9},{9,8},{10,11... | collective-permute-start | bytes 1572872 | tf_op jit(solution)/shard_map/ppermute | solution.py:16
  467.6 25.8 %collective-permute-start.31 = (bf16[32,64,128]{2,1,0:T(8,128)(2,1)}, bf16[32,64,128]{2,1,0:T(8,128)(2,1)}, u32[]{:S(2)}, u32[]{:S(2)}) collective-permute-start(bf16[32,64,128]{2,1,0:T(8,128)(2,1)} %get-tuple-element.47), channel_id=1, source_target_pairs={{0,2},{1,3},{2,0},{3,1},{4,6},{5,7},{6,4},{7,5},{8,10},{9,11},{10,... | collective-permute-start | bytes 1572872 | tf_op jit(solution)/shard_map/ppermute | solution.py:16
  467.9 26.8 %collective-permute-start.32 = (bf16[32,64,128]{2,1,0:T(8,128)(2,1)}, bf16[32,64,128]{2,1,0:T(8,128)(2,1)S(1)}, u32[]{:S(2)}, u32[]{:S(2)}) collective-permute-start(bf16[32,64,128]{2,1,0:T(8,128)(2,1)} %get-tuple-element.48), channel_id=1, source_target_pairs={{0,3},{1,2},{2,1},{3,0},{4,7},{5,6},{6,5},{7,4},{8,11},{9,10},{10,... | collective-permute-start | bytes 1572872 | tf_op jit(solution)/shard_map/ppermute | solution.py:16
  477.4 25.9 %collective-permute-start.34 = (bf16[32,64,128]{2,1,0:T(8,128)(2,1)}, bf16[32,64,128]{2,1,0:T(8,128)(2,1)S(1)}, u32[]{:S(2)}, u32[]{:S(2)}) collective-permute-start(bf16[32,64,128]{2,1,0:T(8,128)(2,1)} %get-tuple-element.50), channel_id=1, source_target_pairs={{0,5},{1,4},{2,7},{3,6},{4,1},{5,0},{6,3},{7,2},{8,13},{9,12},{10,... | collective-permute-start | bytes 1572872 | tf_op jit(solution)/shard_map/ppermute | solution.py:16
  493.4 32.3 %collective-permute-start.36 = (bf16[32,64,128]{2,1,0:T(8,128)(2,1)}, bf16[32,64,128]{2,1,0:T(8,128)(2,1)S(1)}, u32[]{:S(2)}, u32[]{:S(2)}) collective-permute-start(bf16[32,64,128]{2,1,0:T(8,128)(2,1)} %get-tuple-element.52), channel_id=1, source_target_pairs={{0,7},{1,6},{2,5},{3,4},{4,3},{5,2},{6,1},{7,0},{8,15},{9,14},{10,... | collective-permute-start | bytes 1572872 | tf_op jit(solution)/shard_map/ppermute | solution.py:16
  494.7 31.0 %collective-permute-start.21 = (bf16[32,64,128]{2,1,0:T(8,128)(2,1)}, bf16[32,64,128]{2,1,0:T(8,128)(2,1)S(1)}, u32[]{:S(2)}, u32[]{:S(2)}) collective-permute-start(bf16[32,64,128]{2,1,0:T(8,128)(2,1)} %get-tuple-element.38), channel_id=1, source_target_pairs={{0,1},{1,0},{2,3},{3,2},{4,5},{5,4},{6,7},{7,6},{8,9},{9,8},{10,11... | collective-permute-start | bytes 1572872 | tf_op jit(solution)/shard_map/ppermute | solution.py:16
  495.2 36.2 %collective-permute-start.22 = (bf16[32,64,128]{2,1,0:T(8,128)(2,1)}, bf16[32,64,128]{2,1,0:T(8,128)(2,1)S(1)}, u32[]{:S(2)}, u32[]{:S(2)}) collective-permute-start(bf16[32,64,128]{2,1,0:T(8,128)(2,1)} %get-tuple-element.39), channel_id=1, source_target_pairs={{0,2},{1,3},{2,0},{3,1},{4,6},{5,7},{6,4},{7,5},{8,10},{9,11},{10,... | collective-permute-start | bytes 1572872 | tf_op jit(solution)/shard_map/ppermute | solution.py:16
  503.4 39.8 %collective-permute-start.23 = (bf16[32,64,128]{2,1,0:T(8,128)(2,1)}, bf16[32,64,128]{2,1,0:T(8,128)(2,1)}, u32[]{:S(2)}, u32[]{:S(2)}) collective-permute-start(bf16[32,64,128]{2,1,0:T(8,128)(2,1)} %get-tuple-element.40), channel_id=1, source_target_pairs={{0,3},{1,2},{2,1},{3,0},{4,7},{5,6},{6,5},{7,4},{8,11},{9,10},{10,... | collective-permute-start | bytes 1572872 | tf_op jit(solution)/shard_map/ppermute | solution.py:16
  510.8 32.4 %collective-permute-start.24 = (bf16[32,64,128]{2,1,0:T(8,128)(2,1)}, bf16[32,64,128]{2,1,0:T(8,128)(2,1)}, u32[]{:S(2)}, u32[]{:S(2)}) collective-permute-start(bf16[32,64,128]{2,1,0:T(8,128)(2,1)} %get-tuple-element.41), channel_id=1, source_target_pairs={{0,4},{1,5},{2,6},{3,7},{4,0},{5,1},{6,2},{7,3},{8,12},{9,13},{10,... | collective-permute-start | bytes 1572872 | tf_op jit(solution)/shard_map/ppermute | solution.py:16
  525.7 30.1 %collective-permute-start.26 = (bf16[32,64,128]{2,1,0:T(8,128)(2,1)}, bf16[32,64,128]{2,1,0:T(8,128)(2,1)}, u32[]{:S(2)}, u32[]{:S(2)}) collective-permute-start(bf16[32,64,128]{2,1,0:T(8,128)(2,1)} %get-tuple-element.43), channel_id=1, source_target_pairs={{0,6},{1,7},{2,4},{3,5},{4,2},{5,3},{6,0},{7,1},{8,14},{9,15},{10,... | collective-permute-start | bytes 1572872 | tf_op jit(solution)/shard_map/ppermute | solution.py:16
  531.4 37.3 %collective-permute-start.27 = (bf16[32,64,128]{2,1,0:T(8,128)(2,1)}, bf16[32,64,128]{2,1,0:T(8,128)(2,1)}, u32[]{:S(2)}, u32[]{:S(2)}) collective-permute-start(bf16[32,64,128]{2,1,0:T(8,128)(2,1)} %get-tuple-element.44), channel_id=1, source_target_pairs={{0,7},{1,6},{2,5},{3,4},{4,3},{5,2},{6,1},{7,0},{8,15},{9,14},{10,... | collective-permute-start | bytes 1572872 | tf_op jit(solution)/shard_map/ppermute | solution.py:16
  (22 other events, 920.3 us)

commit v2 on v1

--- a/solution.py
+++ b/solution.py
@@ -102,7 +102,7 @@
                 copy(at, j).wait()
 
 
-def merge(me, pieces, offsets, half_bit, into):
+def merge(me, pieces, offsets, half_bit, into, total_width):
     count = len(offsets)
     blocks, total_rows, _ = pieces[0].shape
     steps = 2 if total_rows % 32 == 0 else 1
@@ -112,7 +112,7 @@
     more = [] if into is None else [into]
     return pl.pallas_call(
         functools.partial(merge_kernel, offsets, half_bit, aliased),
-        out_shape=jax.ShapeDtypeStruct((total_rows, 2 * count * width), pieces[0].dtype),
+        out_shape=jax.ShapeDtypeStruct((total_rows, total_width), pieces[0].dtype),
         grid_spec=pltpu.PrefetchScalarGridSpec(
             num_scalar_prefetch=1,
             grid=(steps,),
@@ -263,19 +263,28 @@
     ]
 
 
+def plan_of(slab_count, layer_count):
+    log_count = slab_count.bit_length() - 1
+    remote = (layer_count + 1) // 2
+    bits = [section_bit(m, remote, log_count) for m in range(remote)]
+    spread = [b for b in range(log_count) if b != bits[0]]
+    free = [b for b in spread if b not in bits]
+    spread = [b for b in spread if b not in free[-1:]] + free[-1:]
+    offsets = [
+        sum(((j >> i) & 1) << b for i, b in enumerate(spread)) for j in range(slab_count // 2)
+    ]
+    half = len(offsets) // 2
+    chunks = [offsets[:half], offsets[half:]] if free else [offsets]
+    return bits, offsets, chunks
+
+
 def local(activations, weights, biases, columns):
     slab_count, group_count = lax.axis_size("slab"), lax.axis_size("groups")
-    log_count = slab_count.bit_length() - 1
     layer_count, _, blocks, width, _ = weights.shape
     rows = activations.shape[0]
     remote = (layer_count + 1) // 2
-    bits = [section_bit(m, remote, log_count) for m in range(remote)]
+    bits, offsets, chunks = plan_of(slab_count, layer_count)
     first_bit = bits[0]
-    spread = [b for b in range(log_count) if b != first_bit]
-    count = slab_count // 2
-    offsets = [
-        sum(((j >> i) & 1) << b for i, b in enumerate(spread)) for j in range(count)
-    ]
     slab, group = lax.axis_index("slab"), lax.axis_index("groups")
     me = jnp.stack([slab, group]).astype(jnp.int32)
 
@@ -285,9 +294,9 @@
     cols = [one.reshape(-1) for one in (columns, far_columns)]
 
     mine = split(me, activations, offsets, first_bit, blocks)
-    pieces = [mine[0]]
-    for j in range(1, count):
-        pieces.append(swap(mine[j], "slab", offsets[j]))
+    pieces = {0: mine[0]}
+    for offset, piece in zip(offsets[1:], mine[1:]):
+        pieces[offset] = swap(piece, "slab", offset)
 
     part = 2 * blocks // group_count
     parts = weights.reshape(layer_count, group_count, part, width, width)
@@ -309,24 +318,29 @@
     def weights_of(half, layer):
         return [None, None] if half == 0 else far[layer : layer + 2]
 
-    halves = [pieces, pieces]
-    for m in range(remote):
-        last = m == remote - 1
+    output = None
+    for chunk in chunks:
         for half in range(2):
-            other, flip = None, 0
-            if m > 0:
-                other = swap(halves[half], "slab", 1 << bits[m])
-                flip = offsets.index(1 << bits[m])
-            halves[half] = two_layers(
-                cols[half], me, halves[half], other, parts, weights_of(half, 2 * m), bias[half],
-                2 * m, half, rows, count, flip, not last,
+            value = [pieces[offset] for offset in chunk]
+            for m in range(remote):
+                last = m == remote - 1
+                other, flip = None, 0
+                if m > 0:
+                    other = swap(value, "slab", 1 << bits[m])
+                    flip = chunk.index(chunk[0] ^ (1 << bits[m]))
+                value = two_layers(
+                    cols[half], me, value, other, parts, weights_of(half, 2 * m), bias[half],
+                    2 * m, half, rows, len(chunk), flip, not last,
+                )
+            back = []
+            for offset, piece in zip(chunk, value):
+                if offset:
+                    piece = swap(piece, "slab", offset)
+                back.append(piece)
+            output = merge(
+                me, back, chunk, half << first_bit, output,
+                slab_count * blocks * width,
             )
-    output = None
-    for half in range(2):
-        back = [halves[half][0]]
-        for j in range(1, count):
-            back.append(swap(halves[half][j], "slab", offsets[j]))
-        output = merge(me, back, offsets, half << first_bit, output)
     return output
 
 
@@ -338,6 +352,16 @@
         P(None, "slab"),
     )
 
-    return jax.shard_map(
+    step = jax.shard_map(
         local, mesh=mesh, in_specs=placed, out_specs=P(("groups", "slab"), None), check_vma=False
     )
+
+
+    def run(activations, weights, biases, columns):
+        layer_count = weights.shape[0]
+        one = step
+        if len(plan_of(mesh.shape["slab"], layer_count)[2]) == 2 and layer_count == 6:
+            one = step
+        return one(activations, weights, biases, columns)
+
+    return run

time: 574 us -> 554 us (0.965)
  waiting for transfers between devices: 423 us -> 357 us
  Pallas kernels: 94.4 us -> 141 us
    ppermute x37 -> x41, waiting for transfers between devices: 423 us -> 357 us  [swap(): return lax.ppermute(block, axis, [(i, i ^ offset) for i in range(count)])]
    pallas_call x6 -> x12, Pallas kernels: 78.7 us -> 121 us  [two_layers(): pl.pallas_call(functools.partial(layers_kernel, plan), out_shape=out_shap...]
    pallas_call x2 -> x4, Pallas kernels: 8.78 us -> 13.2 us  [merge(): pl.pallas_call(functools.partial(merge_kernel, offsets, half_bit, aliased...]
    ppermute x37 -> x41, starting transfers between devices: 44.7 us -> 41.3 us  [swap(): return lax.ppermute(block, axis, [(i, i ^ offset) for i in range(count)])]
  transfers between devices with their start and end apart: 37 -> 41, of which waited for: 21 -> 16; matrix products, arithmetic and copies ran while one was open for 2% -> 1% of each run, Pallas kernels for 14% -> 25%
where the time goes in v2:
time: 554 us; the launch traced here: 552 us
  waiting for transfers between devices  357 us (64%)
  Pallas kernels  141 us (25%)
  starting transfers between devices  41.3 us (7%)
  local copies, waits for them, and re-layouts  11.8 us (2%)
    ppermute x41, waiting for transfers between devices, swap(): return lax.ppermute(block, axis, [(i, i ^ offset) for i in range(count)])  357 us
    pallas_call x12, Pallas kernels, two_layers(): pl.pallas_call(functools.partial(layers_kernel, plan), out_shape=out_shap...  121 us
    ppermute x41, starting transfers between devices, swap(): return lax.ppermute(block, axis, [(i, i ^ offset) for i in range(count)])  41.3 us
    pallas_call x4, Pallas kernels, merge(): pl.pallas_call(functools.partial(merge_kernel, offsets, half_bit, aliased...  13.2 us
  transfers between devices with their start and end apart: 41, of which 16 were waited for; matrix products, arithmetic and copies ran while one was open for 1% of the time, Pallas kernels for 25%

profile of v2, /device:TPU:1, one launch (start us, length us, event | category | flops | bytes accessed | tf_op | source)
XLA Modules:
  0.0 551.9 jit_solution(1452922574902250758)
XLA Ops:
  0.0 4.1 dynamic-slice_bitcast_fusion.1
  7.9 7.1 %split.1 = (bf16[2,32,64,128]{3,2,1,0:T(8,128)(2,1)}, bf16[2,32,64,128]{3,2,1,0:T(8,128)(2,1)}, bf16[2,32,64,128]{3,2,1,0:T(8,128)(2,1)}, bf16[2,32,64,128]{3,2,...) custom-call(s32[2]{0:T(128)} %pad_add_fusion.me_ref, ...), custom_call_target="tpu_custom_call" | custom-call | bytes 16777216 | tf_op jit(solution)/shard_map/split/pallas_call | solution.py:55
  20.3 77.5 %collective-permute-done = s32[6,32]{1,0:T(8,128)S(1)} collective-permute-done((s32[6,32]{1,0:T(8,128)S(1)}, s32[6,32]{1,0:T(8,128)S(1)}, u32[]{:S(2)}, u32[]{:S(2)}) %collective-permute-start) | collective-permute-done | bytes 800 | tf_op jit(solution)/shard_map/ppermute | solution.py:16
  109.9 57.5 %collective-permute-done.3.refs_2_ = bf16[2,32,64,128]{3,2,1,0:T(8,128)(2,1)} collective-permute-done((bf16[2,32,64,128]{3,2,1,0:T(8,128)(2,1)}, bf16[2,32,64,128]{3,2,1,0:T(8,128)(2,1)}, u32[]{:S(2)}, u32[]{:S(2)}) %collective-permute-start.3) | collective-permute-done | bytes 1048608 | tf_op jit(solution)/shard_map/ppermute | solution.py:16
  167.4 3.6 collective-permute-start.30
  172.4 19.1 %collective-permute-done.4.refs_3_ = bf16[2,32,64,128]{3,2,1,0:T(8,128)(2,1)} collective-permute-done((bf16[2,32,64,128]{3,2,1,0:T(8,128)(2,1)}, bf16[2,32,64,128]{3,2,1,0:T(8,128)(2,1)}, u32[]{:S(2)}, u32[]{:S(2)}) %collective-permute-start.4) | collective-permute-done | bytes 1048608 | tf_op jit(solution)/shard_map/ppermute | solution.py:16
  193.0 10.1 %shard_map.49.refs_0_ = bf16[4,32,64,128]{3,2,1,0:T(8,128)(2,1)} custom-call(s32[192]{0:T(256)} %reshape.42.cols_ref, s32[2]{0:T(128)} %pad_add_fusion.me_ref, bf16[2,32,64,128]{3,2,1,0:T(8,128)(2,1)} %collective-permute-done.1.refs_0_, bf16[2,32,64,128]{3,2,1,0:T(8,128)(2,1)} %collective-permute-done.2.refs_1_, ...), custom_call_target="tpu_custom_call" | custom-call | flops 1073741824 | bytes 10485760 | tf_op jit(solution)/shard_map/pallas_call | solution.py:241
  203.3 10.6 %collective-permute-done.30.refs_3_ = bf16[2,32,64,128]{3,2,1,0:T(8,128)(2,1)} collective-permute-done((bf16[2,32,64,128]{3,2,1,0:T(8,128)(2,1)}, bf16[2,32,64,128]{3,2,1,0:T(8,128)(2,1)}, u32[]{:S(2)}, u32[]{:S(2)}) %collective-permute-start.30) | collective-permute-done | bytes 1048608 | tf_op jit(solution)/shard_map/ppermute | solution.py:16
  213.9 10.1 %shard_map.55.refs_0_ = bf16[4,32,64,128]{3,2,1,0:T(8,128)(2,1)} custom-call(s32[192]{0:T(256)} %reshape.42.cols_ref, s32[2]{0:T(128)} %pad_add_fusion.me_ref, bf16[2,32,64,128]{3,2,1,0:T(8,128)(2,1)} %get-tuple-element.41.refs_0_, bf16[2,32,64,128]{3,2,1,0:T(8,128)(2,1)} %collective-permute-done.28.refs_1_, ...), custom_call_target="tpu_custom_call" | custom-call | flops 1073741824 | bytes 10485760 | tf_op jit(solution)/shard_map/pallas_call | solution.py:241
  227.1 12.2 %collective-permute-done.6.refs_5_ = bf16[1,32,128,128]{3,2,1,0:T(8,128)(2,1)} collective-permute-done((bf16[1,32,128,128]{3,2,1,0:T(8,128)(2,1)}, bf16[1,32,128,128]{3,2,1,0:T(8,128)(2,1)}, u32[]{:S(2)}, u32[]{:S(2)}) %collective-permute-start.6) | collective-permute-done | bytes 1048608 | tf_op jit(solution)/shard_map/ppermute | solution.py:16
  239.3 9.9 %shard_map.52.refs_0_ = bf16[4,32,64,128]{3,2,1,0:T(8,128)(2,1)} custom-call(s32[192]{0:T(256)} %reshape.35.cols_ref, s32[2]{0:T(128)} %pad_add_fusion.me_ref, bf16[2,32,64,128]{3,2,1,0:T(8,128)(2,1)} %get-tuple-element.41.refs_0_, bf16[2,32,64,128]{3,2,1,0:T(8,128)(2,1)} %collective-permute-done.28.refs_1_, ...), custom_call_target="tpu_custom_call" | custom-call | flops 1073741824 | bytes 10485760 | tf_op jit(solution)/shard_map/pallas_call | solution.py:241
  249.4 9.9 %shard_map.46.refs_0_ = bf16[4,32,64,128]{3,2,1,0:T(8,128)(2,1)} custom-call(s32[192]{0:T(256)} %reshape.35.cols_ref, s32[2]{0:T(128)} %pad_add_fusion.me_ref, bf16[2,32,64,128]{3,2,1,0:T(8,128)(2,1)} %collective-permute-done.1.refs_0_, bf16[2,32,64,128]{3,2,1,0:T(8,128)(2,1)} %collective-permute-done.2.refs_1_, ...), custom_call_target="tpu_custom_call" | custom-call | flops 1073741824 | bytes 10485760 | tf_op jit(solution)/shard_map/pallas_call | solution.py:241
  260.6 10.2 %shard_map.50.refs_0_ = bf16[4,32,64,128]{3,2,1,0:T(8,128)(2,1)} custom-call(s32[192]{0:T(256)} %reshape.42.cols_ref, s32[2]{0:T(128)} %pad_add_fusion.me_ref, bf16[4,32,64,128]{3,2,1,0:T(8,128)(2,1)} %shard_map.49.refs_0_, bf16[4,32,64,128]{3,2,1,0:T(8,128)(2,1)} %collective-permute-done.22.refs_1_, bf16[6,64,128,128]{3,2,1,0:T(8,128)(2,1)} %bitcast.23, ...), custom_call_target="tpu_custom_call" | custom-call | flops 1073741824 | bytes 10485760 | tf_op jit(solution)/shard_map/pallas_call | solution.py:241
  270.7 33.3 %collective-permute-done.36.refs_1_ = bf16[4,32,64,128]{3,2,1,0:T(8,128)(2,1)} collective-permute-done((bf16[4,32,64,128]{3,2,1,0:T(8,128)(2,1)}, bf16[4,32,64,128]{3,2,1,0:T(8,128)(2,1)}, u32[]{:S(2)}, u32[]{:S(2)}) %collective-permute-start.36) | collective-permute-done | bytes 2097184 | tf_op jit(solution)/shard_map/ppermute | solution.py:16
  304.0 10.2 %shard_map.56.refs_0_ = bf16[4,32,64,128]{3,2,1,0:T(8,128)(2,1)} custom-call(s32[192]{0:T(256)} %reshape.42.cols_ref, s32[2]{0:T(128)} %pad_add_fusion.me_ref, bf16[4,32,64,128]{3,2,1,0:T(8,128)(2,1)} %shard_map.55.refs_0_, bf16[4,32,64,128]{3,2,1,0:T(8,128)(2,1)} %collective-permute-done.36.refs_1_, bf16[6,64,128,128]{3,2,1,0:T(8,128)(2,1)} %bitcast.25, ...), custom_call_target="tpu_custom_call" | custom-call | flops 1073741824 | bytes 10485760 | tf_op jit(solution)/shard_map/pallas_call | solution.py:241
  314.4 34.5 %collective-permute-done.31.refs_1_ = bf16[4,32,64,128]{3,2,1,0:T(8,128)(2,1)} collective-permute-done((bf16[4,32,64,128]{3,2,1,0:T(8,128)(2,1)}, bf16[4,32,64,128]{3,2,1,0:T(8,128)(2,1)}, u32[]{:S(2)}, u32[]{:S(2)}) %collective-permute-start.31) | collective-permute-done | bytes 2097184 | tf_op jit(solution)/shard_map/ppermute | solution.py:16
  349.0 10.0 %shard_map.53.refs_0_ = bf16[4,32,64,128]{3,2,1,0:T(8,128)(2,1)} custom-call(s32[192]{0:T(256)} %reshape.35.cols_ref, s32[2]{0:T(128)} %pad_add_fusion.me_ref, bf16[4,32,64,128]{3,2,1,0:T(8,128)(2,1)} %shard_map.52.refs_0_, bf16[4,32,64,128]{3,2,1,0:T(8,128)(2,1)} %collective-permute-done.31.refs_1_, bf16[2,32,128,128]{3,2,1,0:T(8,128)(2,1)} %copy-done, ...), custom_call_target="tpu_custom_call" | custom-call | flops 1073741824 | bytes 10485760 | tf_op jit(solution)/shard_map/pallas_call | solution.py:241
  359.0 34.7 %collective-permute-done.10.refs_1_ = bf16[4,32,64,128]{3,2,1,0:T(8,128)(2,1)} collective-permute-done((bf16[4,32,64,128]{3,2,1,0:T(8,128)(2,1)}, bf16[4,32,64,128]{3,2,1,0:T(8,128)(2,1)}, u32[]{:S(2)}, u32[]{:S(2)}) %collective-permute-start.10) | collective-permute-done | bytes 2097184 | tf_op jit(solution)/shard_map/ppermute | solution.py:16
  394.1 10.0 %shard_map.47.refs_0_ = bf16[4,32,64,128]{3,2,1,0:T(8,128)(2,1)} custom-call(s32[192]{0:T(256)} %reshape.35.cols_ref, s32[2]{0:T(128)} %pad_add_fusion.me_ref, bf16[4,32,64,128]{3,2,1,0:T(8,128)(2,1)} %shard_map.46.refs_0_, bf16[4,32,64,128]{3,2,1,0:T(8,128)(2,1)} %collective-permute-done.10.refs_1_, bf16[2,32,128,128]{3,2,1,0:T(8,128)(2,1)} %copy-done, ...), custom_call_target="tpu_custom_call" | custom-call | flops 1073741824 | bytes 10485760 | tf_op jit(solution)/shard_map/pallas_call | solution.py:241
  405.7 10.1 %shard_map.51 = (bf16[32,64,128]{2,1,0:T(8,128)(2,1)}, bf16[32,64,128]{2,1,0:T(8,128)(2,1)}, bf16[32,64,128]{2,1,0:T(8,128)(2,1)}, bf16[32,64,128]{2,1,0:T(8,128)(2,1)}) custom-call(s32[192]{0:T(256)} %reshape.42.cols_ref, s32[2]{0:T(128)} %pad_add_fusion.me_ref, bf16[4,32,64,128]{3,2,1,0:T(8,128)(2,1)} %shard_map.50.refs_0_, ...), custom_call_target="tpu_custom_call" | custom-call | flops 1073741824 | bytes 10485760 | tf_op jit(solution)/shard_map/pallas_call | solution.py:241
  416.0 10.4 %shard_map.57 = (bf16[32,64,128]{2,1,0:T(8,128)(2,1)}, bf16[32,64,128]{2,1,0:T(8,128)(2,1)}, bf16[32,64,128]{2,1,0:T(8,128)(2,1)}, bf16[32,64,128]{2,1,0:T(8,128)(2,1)}) custom-call(s32[192]{0:T(256)} %reshape.42.cols_ref, s32[2]{0:T(128)} %pad_add_fusion.me_ref, bf16[4,32,64,128]{3,2,1,0:T(8,128)(2,1)} %shard_map.56.refs_0_, ...), custom_call_target="tpu_custom_call" | custom-call | flops 1073741824 | bytes 10485760 | tf_op jit(solution)/shard_map/pallas_call | solution.py:241
  429.0 22.1 %collective-permute-done.15.refs_3_ = bf16[1,32,128,128]{3,2,1,0:T(8,128)(2,1)} collective-permute-done((bf16[1,32,128,128]{3,2,1,0:T(8,128)(2,1)S(1)}, bf16[1,32,128,128]{3,2,1,0:T(8,128)(2,1)}, u32[]{:S(2)}, u32[]{:S(2)}) %collective-permute-start.15) | collective-permute-done | bytes 1048608 | tf_op jit(solution)/shard_map/ppermute | solution.py:16
  452.4 10.0 %shard_map.54 = (bf16[32,64,128]{2,1,0:T(8,128)(2,1)}, bf16[32,64,128]{2,1,0:T(8,128)(2,1)}, bf16[32,64,128]{2,1,0:T(8,128)(2,1)}, bf16[32,64,128]{2,1,0:T(8,128)(2,1)}) custom-call(s32[192]{0:T(256)} %reshape.35.cols_ref, s32[2]{0:T(128)} %pad_add_fusion.me_ref, bf16[4,32,64,128]{3,2,1,0:T(8,128)(2,1)} %shard_map.53.refs_0_, ...), custom_call_target="tpu_custom_call" | custom-call | flops 1073741824 | bytes 10485760 | tf_op jit(solution)/shard_map/pallas_call | solution.py:241
  468.4 10.0 %shard_map.48 = (bf16[32,64,128]{2,1,0:T(8,128)(2,1)}, bf16[32,64,128]{2,1,0:T(8,128)(2,1)}, bf16[32,64,128]{2,1,0:T(8,128)(2,1)}, bf16[32,64,128]{2,1,0:T(8,128)(2,1)}) custom-call(s32[192]{0:T(256)} %reshape.35.cols_ref, s32[2]{0:T(128)} %pad_add_fusion.me_ref, bf16[4,32,64,128]{3,2,1,0:T(8,128)(2,1)} %shard_map.47.refs_0_, ...), custom_call_target="tpu_custom_call" | custom-call | flops 1073741824 | bytes 10485760 | tf_op jit(solution)/shard_map/pallas_call | solution.py:241
  480.2 19.8 %collective-permute-done.40.refs_3_ = bf16[32,64,128]{2,1,0:T(8,128)(2,1)} collective-permute-done((bf16[32,64,128]{2,1,0:T(8,128)(2,1)}, bf16[32,64,128]{2,1,0:T(8,128)(2,1)}, u32[]{:S(2)}, u32[]{:S(2)}) %collective-permute-start.40) | collective-permute-done | bytes 524320 | tf_op jit(solution)/shard_map/ppermute | solution.py:16
  502.0 9.1 %collective-permute-done.34.refs_2_ = bf16[32,64,128]{2,1,0:T(8,128)(2,1)S(1)} collective-permute-done((bf16[32,64,128]{2,1,0:T(8,128)(2,1)}, bf16[32,64,128]{2,1,0:T(8,128)(2,1)S(1)}, u32[]{:S(2)}, u32[]{:S(2)}) %collective-permute-start.34) | collective-permute-done | bytes 524320 | tf_op jit(solution)/shard_map/ppermute | solution.py:16
  512.6 9.8 %collective-permute-done.35.refs_3_ = bf16[32,64,128]{2,1,0:T(8,128)(2,1)S(1)} collective-permute-done((bf16[32,64,128]{2,1,0:T(8,128)(2,1)}, bf16[32,64,128]{2,1,0:T(8,128)(2,1)S(1)}, u32[]{:S(2)}, u32[]{:S(2)}) %collective-permute-start.35) | collective-permute-done | bytes 524320 | tf_op jit(solution)/shard_map/ppermute | solution.py:16
  524.1 3.3 shard_map.58.refs_4_
  527.4 3.3 shard_map.59.refs_4_
  531.6 3.3 shard_map.60.refs_4_
  537.2 11.2 %collective-permute-done.21.refs_3_ = bf16[32,64,128]{2,1,0:T(8,128)(2,1)} collective-permute-done((bf16[32,64,128]{2,1,0:T(8,128)(2,1)}, bf16[32,64,128]{2,1,0:T(8,128)(2,1)}, u32[]{:S(2)}, u32[]{:S(2)}) %collective-permute-start.21) | collective-permute-done | bytes 524320 | tf_op jit(solution)/shard_map/ppermute | solution.py:16
  548.4 3.3 shard_map.61
  (108 shorter events, 51.1 us)
Async XLA Ops:
  4.1 99.1 %collective-permute-start.7 = (bf16[1,32,128,128]{3,2,1,0:T(8,128)(2,1)}, bf16[1,32,128,128]{3,2,1,0:T(8,128)(2,1)S(1)}, u32[]{:S(2)}, u32[]{:S(2)}) collective-permute-start(bf16[1,32,128,128]{3,2,1,0:T(8,128)(2,1)} %get-tuple-element.55), channel_id=1, source_target_pairs={{0,8},{1,9},{2,10},{3,11},{4,12},{5,13},{6,14},{7,15},{8,0},{9,1},... | collective-permute-start | bytes 3145736 | tf_op jit(solution)/shard_map/ppermute | solution.py:16
  7.2 97.6 %collective-permute-start.5 = (bf16[1,32,128,128]{3,2,1,0:T(8,128)(2,1)S(1)}, bf16[1,32,128,128]{3,2,1,0:T(8,128)(2,1)S(1)}, u32[]{:S(2)}, u32[]{:S(2)}) collective-permute-start(bf16[1,32,128,128]{3,2,1,0:T(8,128)(2,1)S(1)} %get-tuple-element.56), channel_id=1, source_target_pairs={{0,8},{1,9},{2,10},{3,11},{4,12},{5,13},{6,14},{7,15},{8,0},{9,1},... | collective-permute-start | bytes 3145736 | tf_op jit(solution)/shard_map/ppermute | solution.py:16
  15.0 90.8 %collective-permute-start.1 = (bf16[2,32,64,128]{3,2,1,0:T(8,128)(2,1)}, bf16[2,32,64,128]{3,2,1,0:T(8,128)(2,1)}, u32[]{:S(2)}, u32[]{:S(2)}) collective-permute-start(bf16[2,32,64,128]{3,2,1,0:T(8,128)(2,1)} %get-tuple-element.29), channel_id=1, source_target_pairs={{0,4},{1,5},{2,6},{3,7},{4,0},{5,1},{6,2},{7,3},{8,12},{9,13},{10,... | collective-permute-start | bytes 3145736 | tf_op jit(solution)/shard_map/ppermute | solution.py:16
  16.4 91.8 %collective-permute-start.2 = (bf16[2,32,64,128]{3,2,1,0:T(8,128)(2,1)}, bf16[2,32,64,128]{3,2,1,0:T(8,128)(2,1)}, u32[]{:S(2)}, u32[]{:S(2)}) collective-permute-start(bf16[2,32,64,128]{3,2,1,0:T(8,128)(2,1)} %get-tuple-element.30), channel_id=1, source_target_pairs={{0,5},{1,4},{2,7},{3,6},{4,1},{5,0},{6,3},{7,2},{8,13},{9,12},{10,... | collective-permute-start | bytes 3145736 | tf_op jit(solution)/shard_map/ppermute | solution.py:16
  17.6 80.2 %collective-permute-start = (s32[6,32]{1,0:T(8,128)S(1)}, s32[6,32]{1,0:T(8,128)S(1)}, u32[]{:S(2)}, u32[]{:S(2)}) collective-permute-start(s32[6,32]{1,0:T(8,128)S(1)} %copy-done.16), channel_id=1, source_target_pairs={{0,8},{1,9},{2,10},{3,11},{4,12},{5,13},{6,14},{7,15},{8,0},{9,1},... | collective-permute-start | bytes 2312 | tf_op jit(solution)/shard_map/ppermute | solution.py:16
  97.8 69.6 %collective-permute-start.3 = (bf16[2,32,64,128]{3,2,1,0:T(8,128)(2,1)}, bf16[2,32,64,128]{3,2,1,0:T(8,128)(2,1)}, u32[]{:S(2)}, u32[]{:S(2)}) collective-permute-start(bf16[2,32,64,128]{3,2,1,0:T(8,128)(2,1)} %get-tuple-element.31), channel_id=1, source_target_pairs={{0,6},{1,7},{2,4},{3,5},{4,2},{5,3},{6,0},{7,1},{8,14},{9,15},{10,... | collective-permute-start | bytes 3145736 | tf_op jit(solution)/shard_map/ppermute | solution.py:16
  103.2 88.3 %collective-permute-start.4 = (bf16[2,32,64,128]{3,2,1,0:T(8,128)(2,1)}, bf16[2,32,64,128]{3,2,1,0:T(8,128)(2,1)}, u32[]{:S(2)}, u32[]{:S(2)}) collective-permute-start(bf16[2,32,64,128]{3,2,1,0:T(8,128)(2,1)} %get-tuple-element.32), channel_id=1, source_target_pairs={{0,7},{1,6},{2,5},{3,4},{4,3},{5,2},{6,1},{7,0},{8,15},{9,14},{10,... | collective-permute-start | bytes 3145736 | tf_op jit(solution)/shard_map/ppermute | solution.py:16
  104.8 87.9 %collective-permute-start.28 = (bf16[2,32,64,128]{3,2,1,0:T(8,128)(2,1)}, bf16[2,32,64,128]{3,2,1,0:T(8,128)(2,1)}, u32[]{:S(2)}, u32[]{:S(2)}) collective-permute-start(bf16[2,32,64,128]{3,2,1,0:T(8,128)(2,1)} %get-tuple-element.42), channel_id=1, source_target_pairs={{0,1},{1,0},{2,3},{3,2},{4,5},{5,4},{6,7},{7,6},{8,9},{9,8},{10,11... | collective-permute-start | bytes 3145736 | tf_op jit(solution)/shard_map/ppermute | solution.py:16
  105.8 120.1 %collective-permute-start.11 = (bf16[2,32,128,128]{3,2,1,0:T(8,128)(2,1)}, bf16[2,32,128,128]{3,2,1,0:T(8,128)(2,1)S(1)}, u32[]{:S(2)}, u32[]{:S(2)}) collective-permute-start(bf16[2,32,128,128]{3,2,1,0:T(8,128)(2,1)} %dynamic-slice_bitcast_fusion), channel_id=1, source_target_pairs={{0,8},{1,9},{2,10},{3,11},{4,12},{5,13},{6,14},{7,15},{8,0},{9,1},... | collective-permute-start | bytes 6291464 | tf_op jit(solution)/shard_map/ppermute | solution.py:16
  108.2 94.9 %collective-permute-start.29 = (bf16[2,32,64,128]{3,2,1,0:T(8,128)(2,1)}, bf16[2,32,64,128]{3,2,1,0:T(8,128)(2,1)}, u32[]{:S(2)}, u32[]{:S(2)}) collective-permute-start(bf16[2,32,64,128]{3,2,1,0:T(8,128)(2,1)} %get-tuple-element.43), channel_id=1, source_target_pairs={{0,2},{1,3},{2,0},{3,1},{4,6},{5,7},{6,4},{7,5},{8,10},{9,11},{10,... | collective-permute-start | bytes 3145736 | tf_op jit(solution)/shard_map/ppermute | solution.py:16
  167.4 46.5 %collective-permute-start.30 = (bf16[2,32,64,128]{3,2,1,0:T(8,128)(2,1)}, bf16[2,32,64,128]{3,2,1,0:T(8,128)(2,1)}, u32[]{:S(2)}, u32[]{:S(2)}) collective-permute-start(bf16[2,32,64,128]{3,2,1,0:T(8,128)(2,1)} %get-tuple-element.44), channel_id=1, source_target_pairs={{0,3},{1,2},{2,1},{3,0},{4,7},{5,6},{6,5},{7,4},{8,11},{9,10},{10,... | collective-permute-start | bytes 3145736 | tf_op jit(solution)/shard_map/ppermute | solution.py:16
  191.5 35.6 %collective-permute-start.8 = (bf16[1,32,128,128]{3,2,1,0:T(8,128)(2,1)S(1)}, bf16[1,32,128,128]{3,2,1,0:T(8,128)(2,1)}, u32[]{:S(2)}, u32[]{:S(2)}) collective-permute-start(bf16[1,32,128,128]{3,2,1,0:T(8,128)(2,1)S(1)} %collective-permute-done.7.refs_6_), channel_id=1, source_target_pairs={{0,16},{16,0},{1,17},{17,1},{2,18},{18,2},{3,19},{19,3},{4,20},{20... | collective-permute-start | bytes 3145736 | tf_op jit(solution)/shard_map/ppermute | solution.py:16
  192.7 46.5 %collective-permute-start.6 = (bf16[1,32,128,128]{3,2,1,0:T(8,128)(2,1)}, bf16[1,32,128,128]{3,2,1,0:T(8,128)(2,1)}, u32[]{:S(2)}, u32[]{:S(2)}) collective-permute-start(bf16[1,32,128,128]{3,2,1,0:T(8,128)(2,1)} %copy-done.5), channel_id=1, source_target_pairs={{0,16},{16,0},{1,17},{17,1},{2,18},{18,2},{3,19},{19,3},{4,20},{20... | collective-permute-start | bytes 3145736 | tf_op jit(solution)/shard_map/ppermute | solution.py:16
  203.1 57.5 %collective-permute-start.22 = (bf16[4,32,64,128]{3,2,1,0:T(8,128)(2,1)}, bf16[4,32,64,128]{3,2,1,0:T(8,128)(2,1)}, u32[]{:S(2)}, u32[]{:S(2)}) collective-permute-start(bf16[4,32,64,128]{3,2,1,0:T(8,128)(2,1)} %shard_map.49.refs_0_), channel_id=1, source_target_pairs={{0,2},{1,3},{2,0},{3,1},{4,6},{5,7},{6,4},{7,5},{8,10},{9,11},{10,... | collective-permute-start | bytes 6291464 | tf_op jit(solution)/shard_map/ppermute | solution.py:16
  224.1 79.9 %collective-permute-start.36 = (bf16[4,32,64,128]{3,2,1,0:T(8,128)(2,1)}, bf16[4,32,64,128]{3,2,1,0:T(8,128)(2,1)}, u32[]{:S(2)}, u32[]{:S(2)}) collective-permute-start(bf16[4,32,64,128]{3,2,1,0:T(8,128)(2,1)} %shard_map.55.refs_0_), channel_id=1, source_target_pairs={{0,2},{1,3},{2,0},{3,1},{4,6},{5,7},{6,4},{7,5},{8,10},{9,11},{10,... | collective-permute-start | bytes 6291464 | tf_op jit(solution)/shard_map/ppermute | solution.py:16
  225.8 88.3 %collective-permute-start.12 = (bf16[2,32,128,128]{3,2,1,0:T(8,128)(2,1)S(1)}, bf16[2,32,128,128]{3,2,1,0:T(8,128)(2,1)}, u32[]{:S(2)}, u32[]{:S(2)}) collective-permute-start(bf16[2,32,128,128]{3,2,1,0:T(8,128)(2,1)S(1)} %collective-permute-done.11.refs_2_.refs_4_), channel_id=1, source_target_pairs={{0,16},{16,0},{1,17},{17,1},{2,18},{18,2},{3,19},{19,3},{4,20},{20... | collective-permute-start | bytes 6291464 | tf_op jit(solution)/shard_map/ppermute | solution.py:16
  249.1 99.8 %collective-permute-start.31 = (bf16[4,32,64,128]{3,2,1,0:T(8,128)(2,1)}, bf16[4,32,64,128]{3,2,1,0:T(8,128)(2,1)}, u32[]{:S(2)}, u32[]{:S(2)}) collective-permute-start(bf16[4,32,64,128]{3,2,1,0:T(8,128)(2,1)} %shard_map.52.refs_0_), channel_id=1, source_target_pairs={{0,2},{1,3},{2,0},{3,1},{4,6},{5,7},{6,4},{7,5},{8,10},{9,11},{10,... | collective-permute-start | bytes 6291464 | tf_op jit(solution)/shard_map/ppermute | solution.py:16
  259.2 134.5 %collective-permute-start.10 = (bf16[4,32,64,128]{3,2,1,0:T(8,128)(2,1)}, bf16[4,32,64,128]{3,2,1,0:T(8,128)(2,1)}, u32[]{:S(2)}, u32[]{:S(2)}) collective-permute-start(bf16[4,32,64,128]{3,2,1,0:T(8,128)(2,1)} %shard_map.46.refs_0_), channel_id=1, source_target_pairs={{0,2},{1,3},{2,0},{3,1},{4,6},{5,7},{6,4},{7,5},{8,10},{9,11},{10,... | collective-permute-start | bytes 6291464 | tf_op jit(solution)/shard_map/ppermute | solution.py:16
  270.7 134.8 %collective-permute-start.23 = (bf16[4,32,64,128]{3,2,1,0:T(8,128)(2,1)}, bf16[4,32,64,128]{3,2,1,0:T(8,128)(2,1)}, u32[]{:S(2)}, u32[]{:S(2)}) collective-permute-start(bf16[4,32,64,128]{3,2,1,0:T(8,128)(2,1)} %shard_map.50.refs_0_), channel_id=1, source_target_pairs={{0,1},{1,0},{2,3},{3,2},{4,5},{5,4},{6,7},{7,6},{8,9},{9,8},{10,11... | collective-permute-start | bytes 6291464 | tf_op jit(solution)/shard_map/ppermute | solution.py:16
  304.0 100.1 %collective-permute-start.16 = (bf16[1,32,128,128]{3,2,1,0:T(8,128)(2,1)}, bf16[1,32,128,128]{3,2,1,0:T(8,128)(2,1)S(1)}, u32[]{:S(2)}, u32[]{:S(2)}) collective-permute-start(bf16[1,32,128,128]{3,2,1,0:T(8,128)(2,1)} %get-tuple-element.53), channel_id=1, source_target_pairs={{0,8},{1,9},{2,10},{3,11},{4,12},{5,13},{6,14},{7,15},{8,0},{9,1},... | collective-permute-start | bytes 3145736 | tf_op jit(solution)/shard_map/ppermute | solution.py:16
  314.2 101.7 %collective-permute-start.37 = (bf16[4,32,64,128]{3,2,1,0:T(8,128)(2,1)}, bf16[4,32,64,128]{3,2,1,0:T(8,128)(2,1)}, u32[]{:S(2)}, u32[]{:S(2)}) collective-permute-start(bf16[4,32,64,128]{3,2,1,0:T(8,128)(2,1)} %shard_map.56.refs_0_), channel_id=1, source_target_pairs={{0,1},{1,0},{2,3},{3,2},{4,5},{5,4},{6,7},{7,6},{8,9},{9,8},{10,11... | collective-permute-start | bytes 6291464 | tf_op jit(solution)/shard_map/ppermute | solution.py:16
  349.0 55.3 %collective-permute-start.14 = (bf16[1,32,128,128]{3,2,1,0:T(8,128)(2,1)}, bf16[1,32,128,128]{3,2,1,0:T(8,128)(2,1)S(1)}, u32[]{:S(2)}, u32[]{:S(2)}) collective-permute-start(bf16[1,32,128,128]{3,2,1,0:T(8,128)(2,1)} %get-tuple-element.54), channel_id=1, source_target_pairs={{0,8},{1,9},{2,10},{3,11},{4,12},{5,13},{6,14},{7,15},{8,0},{9,1},... | collective-permute-start | bytes 3145736 | tf_op jit(solution)/shard_map/ppermute | solution.py:16
  393.7 57.5 %collective-permute-start.32 = (bf16[4,32,64,128]{3,2,1,0:T(8,128)(2,1)}, bf16[4,32,64,128]{3,2,1,0:T(8,128)(2,1)}, u32[]{:S(2)}, u32[]{:S(2)}) collective-permute-start(bf16[4,32,64,128]{3,2,1,0:T(8,128)(2,1)} %shard_map.53.refs_0_), channel_id=1, source_target_pairs={{0,1},{1,0},{2,3},{3,2},{4,5},{5,4},{6,7},{7,6},{8,9},{9,8},{10,11... | collective-permute-start | bytes 6291464 | tf_op jit(solution)/shard_map/ppermute | solution.py:16
  404.1 62.8 %collective-permute-start.13 = (bf16[4,32,64,128]{3,2,1,0:T(8,128)(2,1)}, bf16[4,32,64,128]{3,2,1,0:T(8,128)(2,1)}, u32[]{:S(2)}, u32[]{:S(2)}) collective-permute-start(bf16[4,32,64,128]{3,2,1,0:T(8,128)(2,1)} %shard_map.47.refs_0_), channel_id=1, source_target_pairs={{0,1},{1,0},{2,3},{3,2},{4,5},{5,4},{6,7},{7,6},{8,9},{9,8},{10,11... | collective-permute-start | bytes 6291464 | tf_op jit(solution)/shard_map/ppermute | solution.py:16
  405.5 45.7 %collective-permute-start.15 = (bf16[1,32,128,128]{3,2,1,0:T(8,128)(2,1)S(1)}, bf16[1,32,128,128]{3,2,1,0:T(8,128)(2,1)}, u32[]{:S(2)}, u32[]{:S(2)}) collective-permute-start(bf16[1,32,128,128]{3,2,1,0:T(8,128)(2,1)S(1)} %collective-permute-done.14.refs_2_), channel_id=1, source_target_pairs={{0,16},{16,0},{1,17},{17,1},{2,18},{18,2},{3,19},{19,3},{4,20},{20... | collective-permute-start | bytes 3145736 | tf_op jit(solution)/shard_map/ppermute | solution.py:16
  415.9 46.5 %collective-permute-start.24 = (bf16[32,64,128]{2,1,0:T(8,128)(2,1)}, bf16[32,64,128]{2,1,0:T(8,128)(2,1)}, u32[]{:S(2)}, u32[]{:S(2)}) collective-permute-start(bf16[32,64,128]{2,1,0:T(8,128)(2,1)} %get-tuple-element.37), channel_id=1, source_target_pairs={{0,4},{1,5},{2,6},{3,7},{4,0},{5,1},{6,2},{7,3},{8,12},{9,13},{10,... | collective-permute-start | bytes 1572872 | tf_op jit(solution)/shard_map/ppermute | solution.py:16
  462.8 37.2 %collective-permute-start.40 = (bf16[32,64,128]{2,1,0:T(8,128)(2,1)}, bf16[32,64,128]{2,1,0:T(8,128)(2,1)}, u32[]{:S(2)}, u32[]{:S(2)}) collective-permute-start(bf16[32,64,128]{2,1,0:T(8,128)(2,1)} %get-tuple-element.52), channel_id=1, source_target_pairs={{0,3},{1,2},{2,1},{3,0},{4,7},{5,6},{6,5},{7,4},{8,11},{9,10},{10,... | collective-permute-start | bytes 1572872 | tf_op jit(solution)/shard_map/ppermute | solution.py:16
  464.5 36.6 %collective-permute-start.33 = (bf16[32,64,128]{2,1,0:T(8,128)(2,1)}, bf16[32,64,128]{2,1,0:T(8,128)(2,1)S(1)}, u32[]{:S(2)}, u32[]{:S(2)}) collective-permute-start(bf16[32,64,128]{2,1,0:T(8,128)(2,1)} %get-tuple-element.46), channel_id=1, source_target_pairs={{0,1},{1,0},{2,3},{3,2},{4,5},{5,4},{6,7},{7,6},{8,9},{9,8},{10,11... | collective-permute-start | bytes 1572872 | tf_op jit(solution)/shard_map/ppermute | solution.py:16
  466.7 44.4 %collective-permute-start.34 = (bf16[32,64,128]{2,1,0:T(8,128)(2,1)}, bf16[32,64,128]{2,1,0:T(8,128)(2,1)S(1)}, u32[]{:S(2)}, u32[]{:S(2)}) collective-permute-start(bf16[32,64,128]{2,1,0:T(8,128)(2,1)} %get-tuple-element.47), channel_id=1, source_target_pairs={{0,2},{1,3},{2,0},{3,1},{4,6},{5,7},{6,4},{7,5},{8,10},{9,11},{10,... | collective-permute-start | bytes 1572872 | tf_op jit(solution)/shard_map/ppermute | solution.py:16
  466.9 55.5 %collective-permute-start.35 = (bf16[32,64,128]{2,1,0:T(8,128)(2,1)}, bf16[32,64,128]{2,1,0:T(8,128)(2,1)S(1)}, u32[]{:S(2)}, u32[]{:S(2)}) collective-permute-start(bf16[32,64,128]{2,1,0:T(8,128)(2,1)} %get-tuple-element.48), channel_id=1, source_target_pairs={{0,3},{1,2},{2,1},{3,0},{4,7},{5,6},{6,5},{7,4},{8,11},{9,10},{10,... | collective-permute-start | bytes 1572872 | tf_op jit(solution)/shard_map/ppermute | solution.py:16
  478.5 52.2 %collective-permute-start.27 = (bf16[32,64,128]{2,1,0:T(8,128)(2,1)}, bf16[32,64,128]{2,1,0:T(8,128)(2,1)S(1)}, u32[]{:S(2)}, u32[]{:S(2)}) collective-permute-start(bf16[32,64,128]{2,1,0:T(8,128)(2,1)} %get-tuple-element.40), channel_id=1, source_target_pairs={{0,7},{1,6},{2,5},{3,4},{4,3},{5,2},{6,1},{7,0},{8,15},{9,14},{10,... | collective-permute-start | bytes 1572872 | tf_op jit(solution)/shard_map/ppermute | solution.py:16
  500.0 34.9 %collective-permute-start.18 = (bf16[32,64,128]{2,1,0:T(8,128)(2,1)}, bf16[32,64,128]{2,1,0:T(8,128)(2,1)S(1)}, u32[]{:S(2)}, u32[]{:S(2)}) collective-permute-start(bf16[32,64,128]{2,1,0:T(8,128)(2,1)} %get-tuple-element.33), channel_id=1, source_target_pairs={{0,4},{1,5},{2,6},{3,7},{4,0},{5,1},{6,2},{7,3},{8,12},{9,13},{10,... | collective-permute-start | bytes 1572872 | tf_op jit(solution)/shard_map/ppermute | solution.py:16
  (26 other events, 571.1 us)

commit v3 on v2

--- a/solution.py
+++ b/solution.py
@@ -66,7 +66,7 @@
             ],
         ),
         cost_estimate=pl.CostEstimate(
-            flops=0, transcendentals=0, bytes_accessed=4 * activations.size
+            flops=0, transcendentals=0, bytes_accessed=8 * count * rows * width
         ),
         name="split",
     )(me, activations)
@@ -105,7 +105,7 @@
 def merge(me, pieces, offsets, half_bit, into, total_width):
     count = len(offsets)
     blocks, total_rows, _ = pieces[0].shape
-    steps = 2 if total_rows % 32 == 0 else 1
+    steps = 4 if total_rows % 64 == 0 else 1
     rows = total_rows // steps
     width = blocks * 128
     aliased = 0 if into is None else 1
@@ -201,7 +201,7 @@
     blocks = biases.shape[1]
     part = weights.shape[2]
     paired = half == 1 and len(far[0][0]) == 2
-    step = min(8, part, blocks)
+    step = min(16, part, blocks)
     steps = blocks // step
 
     def weight_spec(p, which):
@@ -283,7 +283,7 @@
     layer_count, _, blocks, width, _ = weights.shape
     rows = activations.shape[0]
     remote = (layer_count + 1) // 2
-    bits, offsets, chunks = plan_of(slab_count, layer_count)
+    bits, _, chunks = plan_of(slab_count, layer_count)
     first_bit = bits[0]
     slab, group = lax.axis_index("slab"), lax.axis_index("groups")
     me = jnp.stack([slab, group]).astype(jnp.int32)
@@ -293,10 +293,13 @@
     bias = [one.reshape(layer_count, blocks, 1, width) for one in (biases, far_bias)]
     cols = [one.reshape(-1) for one in (columns, far_columns)]
 
-    mine = split(me, activations, offsets, first_bit, blocks)
-    pieces = {0: mine[0]}
-    for offset, piece in zip(offsets[1:], mine[1:]):
-        pieces[offset] = swap(piece, "slab", offset)
+    pieces = {}
+    for chunk in chunks:
+        mine = split(me, activations, chunk, first_bit, blocks)
+        for offset, piece in zip(chunk, mine):
+            if offset:
+                piece = swap(piece, "slab", offset)
+            pieces[offset] = piece
 
     part = 2 * blocks // group_count
     parts = weights.reshape(layer_count, group_count, part, width, width)
@@ -318,8 +321,8 @@
     def weights_of(half, layer):
         return [None, None] if half == 0 else far[layer : layer + 2]
 
-    output = None
-    for chunk in chunks:
+    returned = {}
+    for c, chunk in enumerate(chunks):
         for half in range(2):
             value = [pieces[offset] for offset in chunk]
             for m in range(remote):
@@ -337,10 +340,13 @@
                 if offset:
                     piece = swap(piece, "slab", offset)
                 back.append(piece)
-            output = merge(
-                me, back, chunk, half << first_bit, output,
-                slab_count * blocks * width,
-            )
+            returned[c, half] = back
+    output = None
+    for c, half in sorted(returned, key=lambda key: key == (0, 1)):
+        output = merge(
+            me, returned[c, half], chunks[c], half << first_bit, output,
+            slab_count * blocks * width,
+        )
     return output
 
 

time: 554 us -> 556 us (level)
  waiting for transfers between devices: 357 us -> 374 us
  Pallas kernels: 141 us -> 127 us
    pallas_call x12, Pallas kernels: 121 us -> 101 us  [two_layers(): pl.pallas_call(functools.partial(layers_kernel, plan), out_shape=out_shap...]
    ppermute x41, waiting for transfers between devices: 357 us -> 374 us  [swap(): return lax.ppermute(block, axis, [(i, i ^ offset) for i in range(count)])]
  transfers between devices with their start and end apart: 41 -> 41, of which waited for: 16 -> 19; matrix products, arithmetic and copies ran while one was open for 1% -> 1% of each run, Pallas kernels for 25% -> 22%
where the time goes in v3:
time: 556 us; the launch traced here: 554 us
  waiting for transfers between devices  374 us (67%)
  Pallas kernels  127 us (23%)
  starting transfers between devices  40.9 us (7%)
  local copies, waits for them, and re-layouts  11 us (2%)
    ppermute x41, waiting for transfers between devices, swap(): return lax.ppermute(block, axis, [(i, i ^ offset) for i in range(count)])  374 us
    pallas_call x12, Pallas kernels, two_layers(): pl.pallas_call(functools.partial(layers_kernel, plan), out_shape=out_shap...  101 us
    ppermute x41, starting transfers between devices, swap(): return lax.ppermute(block, axis, [(i, i ^ offset) for i in range(count)])  40.9 us
    pallas_call x4, Pallas kernels, merge(): pl.pallas_call(functools.partial(merge_kernel, offsets, half_bit, aliased...  17.7 us
  transfers between devices with their start and end apart: 41, of which 19 were waited for; matrix products, arithmetic and copies ran while one was open for 1% of the time, Pallas kernels for 22%

profile of v3, /device:TPU:1, one launch (start us, length us, event | category | flops | bytes accessed | tf_op | source)
XLA Modules:
  0.0 554.5 jit_solution(7516316588454276718)
XLA Ops:
  17.4 80.3 %collective-permute-done = s32[6,32]{1,0:T(8,128)S(1)} collective-permute-done((s32[6,32]{1,0:T(8,128)S(1)}, s32[6,32]{1,0:T(8,128)S(1)}, u32[]{:S(2)}, u32[]{:S(2)}) %collective-permute-start) | collective-permute-done | bytes 800 | tf_op jit(solution)/shard_map/ppermute | solution.py:16
  113.2 47.5 %collective-permute-done.22.refs_2_ = bf16[2,32,64,128]{3,2,1,0:T(8,128)(2,1)} collective-permute-done((bf16[2,32,64,128]{3,2,1,0:T(8,128)(2,1)}, bf16[2,32,64,128]{3,2,1,0:T(8,128)(2,1)}, u32[]{:S(2)}, u32[]{:S(2)}) %collective-permute-start.22) | collective-permute-done | bytes 1048608 | tf_op jit(solution)/shard_map/ppermute | solution.py:16
  165.6 19.2 %collective-permute-done.23.refs_3_ = bf16[2,32,64,128]{3,2,1,0:T(8,128)(2,1)} collective-permute-done((bf16[2,32,64,128]{3,2,1,0:T(8,128)(2,1)}, bf16[2,32,64,128]{3,2,1,0:T(8,128)(2,1)}, u32[]{:S(2)}, u32[]{:S(2)}) %collective-permute-start.23) | collective-permute-done | bytes 1048608 | tf_op jit(solution)/shard_map/ppermute | solution.py:16
  186.3 8.4 %shard_map.52.refs_0_ = bf16[4,32,64,128]{3,2,1,0:T(8,128)(2,1)} custom-call(s32[192]{0:T(256)} %reshape.42.cols_ref, s32[2]{0:T(128)} %pad_add_fusion.me_ref, bf16[2,32,64,128]{3,2,1,0:T(8,128)(2,1)} %collective-permute-done.20.refs_0_, bf16[2,32,64,128]{3,2,1,0:T(8,128)(2,1)} %collective-permute-done.21.refs_1_, ...), custom_call_target="tpu_custom_call" | custom-call | flops 1073741824 | bytes 10485760 | tf_op jit(solution)/shard_map/pallas_call | solution.py:241
  194.9 12.3 %collective-permute-done.3.refs_3_ = bf16[2,32,64,128]{3,2,1,0:T(8,128)(2,1)} collective-permute-done((bf16[2,32,64,128]{3,2,1,0:T(8,128)(2,1)}, bf16[2,32,64,128]{3,2,1,0:T(8,128)(2,1)}, u32[]{:S(2)}, u32[]{:S(2)}) %collective-permute-start.3) | collective-permute-done | bytes 1048608 | tf_op jit(solution)/shard_map/ppermute | solution.py:16
  207.2 8.4 %shard_map.55.refs_0_ = bf16[4,32,64,128]{3,2,1,0:T(8,128)(2,1)} custom-call(s32[192]{0:T(256)} %reshape.42.cols_ref, s32[2]{0:T(128)} %pad_add_fusion.me_ref, bf16[2,32,64,128]{3,2,1,0:T(8,128)(2,1)} %get-tuple-element.29.refs_0_, bf16[2,32,64,128]{3,2,1,0:T(8,128)(2,1)} %collective-permute-done.1.refs_1_, ...), custom_call_target="tpu_custom_call" | custom-call | flops 1073741824 | bytes 10485760 | tf_op jit(solution)/shard_map/pallas_call | solution.py:241
  219.2 13.3 %collective-permute-done.5.refs_5_ = bf16[1,32,128,128]{3,2,1,0:T(8,128)(2,1)} collective-permute-done((bf16[1,32,128,128]{3,2,1,0:T(8,128)(2,1)}, bf16[1,32,128,128]{3,2,1,0:T(8,128)(2,1)}, u32[]{:S(2)}, u32[]{:S(2)}) %collective-permute-start.5) | collective-permute-done | bytes 1048608 | tf_op jit(solution)/shard_map/ppermute | solution.py:16
  232.6 8.2 %shard_map.49.refs_0_ = bf16[4,32,64,128]{3,2,1,0:T(8,128)(2,1)} custom-call(s32[192]{0:T(256)} %reshape.35.cols_ref, s32[2]{0:T(128)} %pad_add_fusion.me_ref, bf16[2,32,64,128]{3,2,1,0:T(8,128)(2,1)} %collective-permute-done.20.refs_0_, bf16[2,32,64,128]{3,2,1,0:T(8,128)(2,1)} %collective-permute-done.21.refs_1_, ...), custom_call_target="tpu_custom_call" | custom-call | flops 1073741824 | bytes 10485760 | tf_op jit(solution)/shard_map/pallas_call | solution.py:241
  241.0 8.2 %shard_map.46.refs_0_ = bf16[4,32,64,128]{3,2,1,0:T(8,128)(2,1)} custom-call(s32[192]{0:T(256)} %reshape.35.cols_ref, s32[2]{0:T(128)} %pad_add_fusion.me_ref, bf16[2,32,64,128]{3,2,1,0:T(8,128)(2,1)} %get-tuple-element.29.refs_0_, bf16[2,32,64,128]{3,2,1,0:T(8,128)(2,1)} %collective-permute-done.1.refs_1_, ...), custom_call_target="tpu_custom_call" | custom-call | flops 1073741824 | bytes 10485760 | tf_op jit(solution)/shard_map/pallas_call | solution.py:241
  252.4 8.5 %shard_map.53.refs_0_ = bf16[4,32,64,128]{3,2,1,0:T(8,128)(2,1)} custom-call(s32[192]{0:T(256)} %reshape.42.cols_ref, s32[2]{0:T(128)} %pad_add_fusion.me_ref, bf16[4,32,64,128]{3,2,1,0:T(8,128)(2,1)} %shard_map.52.refs_0_, bf16[4,32,64,128]{3,2,1,0:T(8,128)(2,1)} %collective-permute-done.30.refs_1_, bf16[6,64,128,128]{3,2,1,0:T(8,128)(2,1)} %bitcast.23, ...), custom_call_target="tpu_custom_call" | custom-call | flops 1073741824 | bytes 10485760 | tf_op jit(solution)/shard_map/pallas_call | solution.py:241
  261.0 36.3 %collective-permute-done.36.refs_1_ = bf16[4,32,64,128]{3,2,1,0:T(8,128)(2,1)} collective-permute-done((bf16[4,32,64,128]{3,2,1,0:T(8,128)(2,1)}, bf16[4,32,64,128]{3,2,1,0:T(8,128)(2,1)}, u32[]{:S(2)}, u32[]{:S(2)}) %collective-permute-start.36) | collective-permute-done | bytes 2097184 | tf_op jit(solution)/shard_map/ppermute | solution.py:16
  297.3 8.7 %shard_map.56.refs_0_ = bf16[4,32,64,128]{3,2,1,0:T(8,128)(2,1)} custom-call(s32[192]{0:T(256)} %reshape.42.cols_ref, s32[2]{0:T(128)} %pad_add_fusion.me_ref, bf16[4,32,64,128]{3,2,1,0:T(8,128)(2,1)} %shard_map.55.refs_0_, bf16[4,32,64,128]{3,2,1,0:T(8,128)(2,1)} %collective-permute-done.36.refs_1_, bf16[6,64,128,128]{3,2,1,0:T(8,128)(2,1)} %bitcast.25, ...), custom_call_target="tpu_custom_call" | custom-call | flops 1073741824 | bytes 10485760 | tf_op jit(solution)/shard_map/pallas_call | solution.py:241
  308.4 33.8 %collective-permute-done.24.refs_1_ = bf16[4,32,64,128]{3,2,1,0:T(8,128)(2,1)} collective-permute-done((bf16[4,32,64,128]{3,2,1,0:T(8,128)(2,1)}, bf16[4,32,64,128]{3,2,1,0:T(8,128)(2,1)}, u32[]{:S(2)}, u32[]{:S(2)}) %collective-permute-start.24) | collective-permute-done | bytes 2097184 | tf_op jit(solution)/shard_map/ppermute | solution.py:16
  342.5 8.4 %shard_map.50.refs_0_ = bf16[4,32,64,128]{3,2,1,0:T(8,128)(2,1)} custom-call(s32[192]{0:T(256)} %reshape.35.cols_ref, s32[2]{0:T(128)} %pad_add_fusion.me_ref, bf16[4,32,64,128]{3,2,1,0:T(8,128)(2,1)} %shard_map.49.refs_0_, bf16[4,32,64,128]{3,2,1,0:T(8,128)(2,1)} %collective-permute-done.24.refs_1_, bf16[2,32,128,128]{3,2,1,0:T(8,128)(2,1)} %copy-done, ...), custom_call_target="tpu_custom_call" | custom-call | flops 1073741824 | bytes 10485760 | tf_op jit(solution)/shard_map/pallas_call | solution.py:241
  350.9 36.1 %collective-permute-done.9.refs_1_ = bf16[4,32,64,128]{3,2,1,0:T(8,128)(2,1)} collective-permute-done((bf16[4,32,64,128]{3,2,1,0:T(8,128)(2,1)}, bf16[4,32,64,128]{3,2,1,0:T(8,128)(2,1)}, u32[]{:S(2)}, u32[]{:S(2)}) %collective-permute-start.9) | collective-permute-done | bytes 2097184 | tf_op jit(solution)/shard_map/ppermute | solution.py:16
  387.4 8.4 %shard_map.47.refs_0_ = bf16[4,32,64,128]{3,2,1,0:T(8,128)(2,1)} custom-call(s32[192]{0:T(256)} %reshape.35.cols_ref, s32[2]{0:T(128)} %pad_add_fusion.me_ref, bf16[4,32,64,128]{3,2,1,0:T(8,128)(2,1)} %shard_map.46.refs_0_, bf16[4,32,64,128]{3,2,1,0:T(8,128)(2,1)} %collective-permute-done.9.refs_1_, bf16[2,32,128,128]{3,2,1,0:T(8,128)(2,1)} %copy-done, ...), custom_call_target="tpu_custom_call" | custom-call | flops 1073741824 | bytes 10485760 | tf_op jit(solution)/shard_map/pallas_call | solution.py:241
  397.5 8.5 %shard_map.54 = (bf16[32,64,128]{2,1,0:T(8,128)(2,1)}, bf16[32,64,128]{2,1,0:T(8,128)(2,1)}, bf16[32,64,128]{2,1,0:T(8,128)(2,1)}, bf16[32,64,128]{2,1,0:T(8,128)(2,1)}) custom-call(s32[192]{0:T(256)} %reshape.42.cols_ref, s32[2]{0:T(128)} %pad_add_fusion.me_ref, bf16[4,32,64,128]{3,2,1,0:T(8,128)(2,1)} %shard_map.53.refs_0_, ...), custom_call_target="tpu_custom_call" | custom-call | flops 1073741824 | bytes 10485760 | tf_op jit(solution)/shard_map/pallas_call | solution.py:241
  406.0 14.4 %collective-permute-done.16.refs_5_ = bf16[1,32,128,128]{3,2,1,0:T(8,128)(2,1)S(1)} collective-permute-done((bf16[1,32,128,128]{3,2,1,0:T(8,128)(2,1)S(1)}, bf16[1,32,128,128]{3,2,1,0:T(8,128)(2,1)S(1)}, u32[]{:S(2)}, u32[]{:S(2)}) %collective-permute-start.16) | collective-permute-done | bytes 1048608 | tf_op jit(solution)/shard_map/ppermute | solution.py:16
  420.3 22.6 %collective-permute-done.14.refs_3_ = bf16[1,32,128,128]{3,2,1,0:T(8,128)(2,1)} collective-permute-done((bf16[1,32,128,128]{3,2,1,0:T(8,128)(2,1)S(1)}, bf16[1,32,128,128]{3,2,1,0:T(8,128)(2,1)}, u32[]{:S(2)}, u32[]{:S(2)}) %collective-permute-start.14) | collective-permute-done | bytes 1048608 | tf_op jit(solution)/shard_map/ppermute | solution.py:16
  446.7 8.5 %shard_map.57 = (bf16[32,64,128]{2,1,0:T(8,128)(2,1)}, bf16[32,64,128]{2,1,0:T(8,128)(2,1)}, bf16[32,64,128]{2,1,0:T(8,128)(2,1)}, bf16[32,64,128]{2,1,0:T(8,128)(2,1)}) custom-call(s32[192]{0:T(256)} %reshape.42.cols_ref, s32[2]{0:T(128)} %pad_add_fusion.me_ref, bf16[4,32,64,128]{3,2,1,0:T(8,128)(2,1)} %shard_map.56.refs_0_, ...), custom_call_target="tpu_custom_call" | custom-call | flops 1073741824 | bytes 10485760 | tf_op jit(solution)/shard_map/pallas_call | solution.py:241
  455.2 8.4 %shard_map.51 = (bf16[32,64,128]{2,1,0:T(8,128)(2,1)}, bf16[32,64,128]{2,1,0:T(8,128)(2,1)}, bf16[32,64,128]{2,1,0:T(8,128)(2,1)}, bf16[32,64,128]{2,1,0:T(8,128)(2,1)}) custom-call(s32[192]{0:T(256)} %reshape.35.cols_ref, s32[2]{0:T(128)} %pad_add_fusion.me_ref, bf16[4,32,64,128]{3,2,1,0:T(8,128)(2,1)} %shard_map.50.refs_0_, ...), custom_call_target="tpu_custom_call" | custom-call | flops 1073741824 | bytes 10485760 | tf_op jit(solution)/shard_map/pallas_call | solution.py:241
  464.2 5.0 collective-permute-done.34.refs_2_
  469.9 9.6 %collective-permute-done.35.refs_3_ = bf16[32,64,128]{2,1,0:T(8,128)(2,1)S(1)} collective-permute-done((bf16[32,64,128]{2,1,0:T(8,128)(2,1)}, bf16[32,64,128]{2,1,0:T(8,128)(2,1)S(1)}, u32[]{:S(2)}, u32[]{:S(2)}) %collective-permute-start.35) | collective-permute-done | bytes 524320 | tf_op jit(solution)/shard_map/ppermute | solution.py:16
  482.2 8.4 %shard_map.48 = (bf16[32,64,128]{2,1,0:T(8,128)(2,1)}, bf16[32,64,128]{2,1,0:T(8,128)(2,1)}, bf16[32,64,128]{2,1,0:T(8,128)(2,1)}, bf16[32,64,128]{2,1,0:T(8,128)(2,1)}) custom-call(s32[192]{0:T(256)} %reshape.35.cols_ref, s32[2]{0:T(128)} %pad_add_fusion.me_ref, bf16[4,32,64,128]{3,2,1,0:T(8,128)(2,1)} %shard_map.47.refs_0_, ...), custom_call_target="tpu_custom_call" | custom-call | flops 1073741824 | bytes 10485760 | tf_op jit(solution)/shard_map/pallas_call | solution.py:241
  492.4 10.1 %collective-permute-done.40.refs_3_ = bf16[32,64,128]{2,1,0:T(8,128)(2,1)} collective-permute-done((bf16[32,64,128]{2,1,0:T(8,128)(2,1)}, bf16[32,64,128]{2,1,0:T(8,128)(2,1)}, u32[]{:S(2)}, u32[]{:S(2)}) %collective-permute-start.40) | collective-permute-done | bytes 524320 | tf_op jit(solution)/shard_map/ppermute | solution.py:16
  506.1 4.4 shard_map.58.refs_4_
  510.5 4.4 shard_map.59.refs_4_
  515.7 12.5 %collective-permute-done.29.refs_3_ = bf16[32,64,128]{2,1,0:T(8,128)(2,1)S(1)} collective-permute-done((bf16[32,64,128]{2,1,0:T(8,128)(2,1)}, bf16[32,64,128]{2,1,0:T(8,128)(2,1)S(1)}, u32[]{:S(2)}, u32[]{:S(2)}) %collective-permute-start.29) | collective-permute-done | bytes 524320 | tf_op jit(solution)/shard_map/ppermute | solution.py:16
  529.0 4.4 shard_map.60.refs_4_
  533.4 5.2 collective-permute-done.18.refs_2_
  538.5 11.3 %collective-permute-done.19.refs_3_ = bf16[32,64,128]{2,1,0:T(8,128)(2,1)} collective-permute-done((bf16[32,64,128]{2,1,0:T(8,128)(2,1)}, bf16[32,64,128]{2,1,0:T(8,128)(2,1)}, u32[]{:S(2)}, u32[]{:S(2)}) %collective-permute-start.19) | collective-permute-done | bytes 524320 | tf_op jit(solution)/shard_map/ppermute | solution.py:16
  549.9 4.4 shard_map.61
  (111 shorter events, 65.8 us)
Async XLA Ops:
  3.9 100.2 %collective-permute-start.6 = (bf16[1,32,128,128]{3,2,1,0:T(8,128)(2,1)}, bf16[1,32,128,128]{3,2,1,0:T(8,128)(2,1)S(1)}, u32[]{:S(2)}, u32[]{:S(2)}) collective-permute-start(bf16[1,32,128,128]{3,2,1,0:T(8,128)(2,1)} %get-tuple-element.55), channel_id=1, source_target_pairs={{0,8},{1,9},{2,10},{3,11},{4,12},{5,13},{6,14},{7,15},{8,0},{9,1},... | collective-permute-start | bytes 3145736 | tf_op jit(solution)/shard_map/ppermute | solution.py:16
  7.1 98.8 %collective-permute-start.4 = (bf16[1,32,128,128]{3,2,1,0:T(8,128)(2,1)S(1)}, bf16[1,32,128,128]{3,2,1,0:T(8,128)(2,1)S(1)}, u32[]{:S(2)}, u32[]{:S(2)}) collective-permute-start(bf16[1,32,128,128]{3,2,1,0:T(8,128)(2,1)S(1)} %get-tuple-element.56), channel_id=1, source_target_pairs={{0,8},{1,9},{2,10},{3,11},{4,12},{5,13},{6,14},{7,15},{8,0},{9,1},... | collective-permute-start | bytes 3145736 | tf_op jit(solution)/shard_map/ppermute | solution.py:16
  12.1 97.4 %collective-permute-start.20 = (bf16[2,32,64,128]{3,2,1,0:T(8,128)(2,1)}, bf16[2,32,64,128]{3,2,1,0:T(8,128)(2,1)}, u32[]{:S(2)}, u32[]{:S(2)}) collective-permute-start(bf16[2,32,64,128]{3,2,1,0:T(8,128)(2,1)} %get-tuple-element.37), channel_id=1, source_target_pairs={{0,4},{1,5},{2,6},{3,7},{4,0},{5,1},{6,2},{7,3},{8,12},{9,13},{10,... | collective-permute-start | bytes 3145736 | tf_op jit(solution)/shard_map/ppermute | solution.py:16
  13.5 98.4 %collective-permute-start.21 = (bf16[2,32,64,128]{3,2,1,0:T(8,128)(2,1)}, bf16[2,32,64,128]{3,2,1,0:T(8,128)(2,1)}, u32[]{:S(2)}, u32[]{:S(2)}) collective-permute-start(bf16[2,32,64,128]{3,2,1,0:T(8,128)(2,1)} %get-tuple-element.38), channel_id=1, source_target_pairs={{0,5},{1,4},{2,7},{3,6},{4,1},{5,0},{6,3},{7,2},{8,13},{9,12},{10,... | collective-permute-start | bytes 3145736 | tf_op jit(solution)/shard_map/ppermute | solution.py:16
  14.8 82.9 %collective-permute-start = (s32[6,32]{1,0:T(8,128)S(1)}, s32[6,32]{1,0:T(8,128)S(1)}, u32[]{:S(2)}, u32[]{:S(2)}) collective-permute-start(s32[6,32]{1,0:T(8,128)S(1)} %copy-done.17), channel_id=1, source_target_pairs={{0,8},{1,9},{2,10},{3,11},{4,12},{5,13},{6,14},{7,15},{8,0},{9,1},... | collective-permute-start | bytes 2312 | tf_op jit(solution)/shard_map/ppermute | solution.py:16
  97.7 63.0 %collective-permute-start.22 = (bf16[2,32,64,128]{3,2,1,0:T(8,128)(2,1)}, bf16[2,32,64,128]{3,2,1,0:T(8,128)(2,1)}, u32[]{:S(2)}, u32[]{:S(2)}) collective-permute-start(bf16[2,32,64,128]{3,2,1,0:T(8,128)(2,1)} %get-tuple-element.39), channel_id=1, source_target_pairs={{0,6},{1,7},{2,4},{3,5},{4,2},{5,3},{6,0},{7,1},{8,14},{9,15},{10,... | collective-permute-start | bytes 3145736 | tf_op jit(solution)/shard_map/ppermute | solution.py:16
  104.2 80.6 %collective-permute-start.23 = (bf16[2,32,64,128]{3,2,1,0:T(8,128)(2,1)}, bf16[2,32,64,128]{3,2,1,0:T(8,128)(2,1)}, u32[]{:S(2)}, u32[]{:S(2)}) collective-permute-start(bf16[2,32,64,128]{3,2,1,0:T(8,128)(2,1)} %get-tuple-element.40), channel_id=1, source_target_pairs={{0,7},{1,6},{2,5},{3,4},{4,3},{5,2},{6,1},{7,0},{8,15},{9,14},{10,... | collective-permute-start | bytes 3145736 | tf_op jit(solution)/shard_map/ppermute | solution.py:16
  105.9 80.1 %collective-permute-start.1 = (bf16[2,32,64,128]{3,2,1,0:T(8,128)(2,1)}, bf16[2,32,64,128]{3,2,1,0:T(8,128)(2,1)}, u32[]{:S(2)}, u32[]{:S(2)}) collective-permute-start(bf16[2,32,64,128]{3,2,1,0:T(8,128)(2,1)} %get-tuple-element.30), channel_id=1, source_target_pairs={{0,1},{1,0},{2,3},{3,2},{4,5},{5,4},{6,7},{7,6},{8,9},{9,8},{10,11... | collective-permute-start | bytes 3145736 | tf_op jit(solution)/shard_map/ppermute | solution.py:16
  109.5 108.4 %collective-permute-start.10 = (bf16[2,32,128,128]{3,2,1,0:T(8,128)(2,1)}, bf16[2,32,128,128]{3,2,1,0:T(8,128)(2,1)S(1)}, u32[]{:S(2)}, u32[]{:S(2)}) collective-permute-start(bf16[2,32,128,128]{3,2,1,0:T(8,128)(2,1)} %dynamic-slice_bitcast_fusion), channel_id=1, source_target_pairs={{0,8},{1,9},{2,10},{3,11},{4,12},{5,13},{6,14},{7,15},{8,0},{9,1},... | collective-permute-start | bytes 6291464 | tf_op jit(solution)/shard_map/ppermute | solution.py:16
  111.9 82.8 %collective-permute-start.2 = (bf16[2,32,64,128]{3,2,1,0:T(8,128)(2,1)}, bf16[2,32,64,128]{3,2,1,0:T(8,128)(2,1)}, u32[]{:S(2)}, u32[]{:S(2)}) collective-permute-start(bf16[2,32,64,128]{3,2,1,0:T(8,128)(2,1)} %get-tuple-element.31), channel_id=1, source_target_pairs={{0,2},{1,3},{2,0},{3,1},{4,6},{5,7},{6,4},{7,5},{8,10},{9,11},{10,... | collective-permute-start | bytes 3145736 | tf_op jit(solution)/shard_map/ppermute | solution.py:16
  160.7 46.5 %collective-permute-start.3 = (bf16[2,32,64,128]{3,2,1,0:T(8,128)(2,1)}, bf16[2,32,64,128]{3,2,1,0:T(8,128)(2,1)}, u32[]{:S(2)}, u32[]{:S(2)}) collective-permute-start(bf16[2,32,64,128]{3,2,1,0:T(8,128)(2,1)} %get-tuple-element.32), channel_id=1, source_target_pairs={{0,3},{1,2},{2,1},{3,0},{4,7},{5,6},{6,5},{7,4},{8,11},{9,10},{10,... | collective-permute-start | bytes 3145736 | tf_op jit(solution)/shard_map/ppermute | solution.py:16
  184.8 34.4 %collective-permute-start.7 = (bf16[1,32,128,128]{3,2,1,0:T(8,128)(2,1)S(1)}, bf16[1,32,128,128]{3,2,1,0:T(8,128)(2,1)}, u32[]{:S(2)}, u32[]{:S(2)}) collective-permute-start(bf16[1,32,128,128]{3,2,1,0:T(8,128)(2,1)S(1)} %collective-permute-done.6.refs_6_), channel_id=1, source_target_pairs={{0,16},{16,0},{1,17},{17,1},{2,18},{18,2},{3,19},{19,3},{4,20},{20... | collective-permute-start | bytes 3145736 | tf_op jit(solution)/shard_map/ppermute | solution.py:16
  186.0 46.5 %collective-permute-start.5 = (bf16[1,32,128,128]{3,2,1,0:T(8,128)(2,1)}, bf16[1,32,128,128]{3,2,1,0:T(8,128)(2,1)}, u32[]{:S(2)}, u32[]{:S(2)}) collective-permute-start(bf16[1,32,128,128]{3,2,1,0:T(8,128)(2,1)} %copy-done.5), channel_id=1, source_target_pairs={{0,16},{16,0},{1,17},{17,1},{2,18},{18,2},{3,19},{19,3},{4,20},{20... | collective-permute-start | bytes 3145736 | tf_op jit(solution)/shard_map/ppermute | solution.py:16
  194.7 57.7 %collective-permute-start.30 = (bf16[4,32,64,128]{3,2,1,0:T(8,128)(2,1)}, bf16[4,32,64,128]{3,2,1,0:T(8,128)(2,1)}, u32[]{:S(2)}, u32[]{:S(2)}) collective-permute-start(bf16[4,32,64,128]{3,2,1,0:T(8,128)(2,1)} %shard_map.52.refs_0_), channel_id=1, source_target_pairs={{0,2},{1,3},{2,0},{3,1},{4,6},{5,7},{6,4},{7,5},{8,10},{9,11},{10,... | collective-permute-start | bytes 6291464 | tf_op jit(solution)/shard_map/ppermute | solution.py:16
  215.7 81.6 %collective-permute-start.36 = (bf16[4,32,64,128]{3,2,1,0:T(8,128)(2,1)}, bf16[4,32,64,128]{3,2,1,0:T(8,128)(2,1)}, u32[]{:S(2)}, u32[]{:S(2)}) collective-permute-start(bf16[4,32,64,128]{3,2,1,0:T(8,128)(2,1)} %shard_map.55.refs_0_), channel_id=1, source_target_pairs={{0,2},{1,3},{2,0},{3,1},{4,6},{5,7},{6,4},{7,5},{8,10},{9,11},{10,... | collective-permute-start | bytes 6291464 | tf_op jit(solution)/shard_map/ppermute | solution.py:16
  217.9 88.1 %collective-permute-start.11 = (bf16[2,32,128,128]{3,2,1,0:T(8,128)(2,1)S(1)}, bf16[2,32,128,128]{3,2,1,0:T(8,128)(2,1)}, u32[]{:S(2)}, u32[]{:S(2)}) collective-permute-start(bf16[2,32,128,128]{3,2,1,0:T(8,128)(2,1)S(1)} %collective-permute-done.10.refs_2_.refs_4_), channel_id=1, source_target_pairs={{0,16},{16,0},{1,17},{17,1},{2,18},{18,2},{3,19},{19,3},{4,20},{20... | collective-permute-start | bytes 6291464 | tf_op jit(solution)/shard_map/ppermute | solution.py:16
  240.8 101.4 %collective-permute-start.24 = (bf16[4,32,64,128]{3,2,1,0:T(8,128)(2,1)}, bf16[4,32,64,128]{3,2,1,0:T(8,128)(2,1)}, u32[]{:S(2)}, u32[]{:S(2)}) collective-permute-start(bf16[4,32,64,128]{3,2,1,0:T(8,128)(2,1)} %shard_map.49.refs_0_), channel_id=1, source_target_pairs={{0,2},{1,3},{2,0},{3,1},{4,6},{5,7},{6,4},{7,5},{8,10},{9,11},{10,... | collective-permute-start | bytes 6291464 | tf_op jit(solution)/shard_map/ppermute | solution.py:16
  249.2 137.8 %collective-permute-start.9 = (bf16[4,32,64,128]{3,2,1,0:T(8,128)(2,1)}, bf16[4,32,64,128]{3,2,1,0:T(8,128)(2,1)}, u32[]{:S(2)}, u32[]{:S(2)}) collective-permute-start(bf16[4,32,64,128]{3,2,1,0:T(8,128)(2,1)} %shard_map.46.refs_0_), channel_id=1, source_target_pairs={{0,2},{1,3},{2,0},{3,1},{4,6},{5,7},{6,4},{7,5},{8,10},{9,11},{10,... | collective-permute-start | bytes 6291464 | tf_op jit(solution)/shard_map/ppermute | solution.py:16
  260.8 136.4 %collective-permute-start.31 = (bf16[4,32,64,128]{3,2,1,0:T(8,128)(2,1)}, bf16[4,32,64,128]{3,2,1,0:T(8,128)(2,1)}, u32[]{:S(2)}, u32[]{:S(2)}) collective-permute-start(bf16[4,32,64,128]{3,2,1,0:T(8,128)(2,1)} %shard_map.53.refs_0_), channel_id=1, source_target_pairs={{0,1},{1,0},{2,3},{3,2},{4,5},{5,4},{6,7},{7,6},{8,9},{9,8},{10,11... | collective-permute-start | bytes 6291464 | tf_op jit(solution)/shard_map/ppermute | solution.py:16
  297.3 98.5 %collective-permute-start.15 = (bf16[1,32,128,128]{3,2,1,0:T(8,128)(2,1)}, bf16[1,32,128,128]{3,2,1,0:T(8,128)(2,1)S(1)}, u32[]{:S(2)}, u32[]{:S(2)}) collective-permute-start(bf16[1,32,128,128]{3,2,1,0:T(8,128)(2,1)} %get-tuple-element.53), channel_id=1, source_target_pairs={{0,8},{1,9},{2,10},{3,11},{4,12},{5,13},{6,14},{7,15},{8,0},{9,1},... | collective-permute-start | bytes 3145736 | tf_op jit(solution)/shard_map/ppermute | solution.py:16
  306.0 90.0 %collective-permute-start.13 = (bf16[1,32,128,128]{3,2,1,0:T(8,128)(2,1)}, bf16[1,32,128,128]{3,2,1,0:T(8,128)(2,1)S(1)}, u32[]{:S(2)}, u32[]{:S(2)}) collective-permute-start(bf16[1,32,128,128]{3,2,1,0:T(8,128)(2,1)} %get-tuple-element.54), channel_id=1, source_target_pairs={{0,8},{1,9},{2,10},{3,11},{4,12},{5,13},{6,14},{7,15},{8,0},{9,1},... | collective-permute-start | bytes 3145736 | tf_op jit(solution)/shard_map/ppermute | solution.py:16
  342.3 100.7 %collective-permute-start.37 = (bf16[4,32,64,128]{3,2,1,0:T(8,128)(2,1)}, bf16[4,32,64,128]{3,2,1,0:T(8,128)(2,1)}, u32[]{:S(2)}, u32[]{:S(2)}) collective-permute-start(bf16[4,32,64,128]{3,2,1,0:T(8,128)(2,1)} %shard_map.56.refs_0_), channel_id=1, source_target_pairs={{0,1},{1,0},{2,3},{3,2},{4,5},{5,4},{6,7},{7,6},{8,9},{9,8},{10,11... | collective-permute-start | bytes 6291464 | tf_op jit(solution)/shard_map/ppermute | solution.py:16
  387.0 58.5 %collective-permute-start.25 = (bf16[4,32,64,128]{3,2,1,0:T(8,128)(2,1)}, bf16[4,32,64,128]{3,2,1,0:T(8,128)(2,1)}, u32[]{:S(2)}, u32[]{:S(2)}) collective-permute-start(bf16[4,32,64,128]{3,2,1,0:T(8,128)(2,1)} %shard_map.50.refs_0_), channel_id=1, source_target_pairs={{0,1},{1,0},{2,3},{3,2},{4,5},{5,4},{6,7},{7,6},{8,9},{9,8},{10,11... | collective-permute-start | bytes 6291464 | tf_op jit(solution)/shard_map/ppermute | solution.py:16
  395.8 83.7 %collective-permute-start.12 = (bf16[4,32,64,128]{3,2,1,0:T(8,128)(2,1)}, bf16[4,32,64,128]{3,2,1,0:T(8,128)(2,1)}, u32[]{:S(2)}, u32[]{:S(2)}) collective-permute-start(bf16[4,32,64,128]{3,2,1,0:T(8,128)(2,1)} %shard_map.47.refs_0_), channel_id=1, source_target_pairs={{0,1},{1,0},{2,3},{3,2},{4,5},{5,4},{6,7},{7,6},{8,9},{9,8},{10,11... | collective-permute-start | bytes 6291464 | tf_op jit(solution)/shard_map/ppermute | solution.py:16
  397.2 45.7 %collective-permute-start.14 = (bf16[1,32,128,128]{3,2,1,0:T(8,128)(2,1)S(1)}, bf16[1,32,128,128]{3,2,1,0:T(8,128)(2,1)}, u32[]{:S(2)}, u32[]{:S(2)}) collective-permute-start(bf16[1,32,128,128]{3,2,1,0:T(8,128)(2,1)S(1)} %collective-permute-done.13.refs_2_), channel_id=1, source_target_pairs={{0,16},{16,0},{1,17},{17,1},{2,18},{18,2},{3,19},{19,3},{4,20},{20... | collective-permute-start | bytes 3145736 | tf_op jit(solution)/shard_map/ppermute | solution.py:16
  420.3 43.3 %collective-permute-start.32 = (bf16[32,64,128]{2,1,0:T(8,128)(2,1)}, bf16[32,64,128]{2,1,0:T(8,128)(2,1)S(1)}, u32[]{:S(2)}, u32[]{:S(2)}) collective-permute-start(bf16[32,64,128]{2,1,0:T(8,128)(2,1)} %get-tuple-element.45), channel_id=1, source_target_pairs={{0,4},{1,5},{2,6},{3,7},{4,0},{5,1},{6,2},{7,3},{8,12},{9,13},{10,... | collective-permute-start | bytes 1572872 | tf_op jit(solution)/shard_map/ppermute | solution.py:16
  445.5 34.0 %collective-permute-start.35 = (bf16[32,64,128]{2,1,0:T(8,128)(2,1)}, bf16[32,64,128]{2,1,0:T(8,128)(2,1)S(1)}, u32[]{:S(2)}, u32[]{:S(2)}) collective-permute-start(bf16[32,64,128]{2,1,0:T(8,128)(2,1)} %get-tuple-element.48), channel_id=1, source_target_pairs={{0,7},{1,6},{2,5},{3,4},{4,3},{5,2},{6,1},{7,0},{8,15},{9,14},{10,... | collective-permute-start | bytes 1572872 | tf_op jit(solution)/shard_map/ppermute | solution.py:16
  469.2 33.3 %collective-permute-start.40 = (bf16[32,64,128]{2,1,0:T(8,128)(2,1)}, bf16[32,64,128]{2,1,0:T(8,128)(2,1)}, u32[]{:S(2)}, u32[]{:S(2)}) collective-permute-start(bf16[32,64,128]{2,1,0:T(8,128)(2,1)} %get-tuple-element.52), channel_id=1, source_target_pairs={{0,3},{1,2},{2,1},{3,0},{4,7},{5,6},{6,5},{7,4},{8,11},{9,10},{10,... | collective-permute-start | bytes 1572872 | tf_op jit(solution)/shard_map/ppermute | solution.py:16
  491.5 36.7 %collective-permute-start.29 = (bf16[32,64,128]{2,1,0:T(8,128)(2,1)}, bf16[32,64,128]{2,1,0:T(8,128)(2,1)S(1)}, u32[]{:S(2)}, u32[]{:S(2)}) collective-permute-start(bf16[32,64,128]{2,1,0:T(8,128)(2,1)} %get-tuple-element.44), channel_id=1, source_target_pairs={{0,7},{1,6},{2,5},{3,4},{4,3},{5,2},{6,1},{7,0},{8,15},{9,14},{10,... | collective-permute-start | bytes 1572872 | tf_op jit(solution)/shard_map/ppermute | solution.py:16
  502.5 30.8 %collective-permute-start.17 = (bf16[32,64,128]{2,1,0:T(8,128)(2,1)}, bf16[32,64,128]{2,1,0:T(8,128)(2,1)S(1)}, u32[]{:S(2)}, u32[]{:S(2)}) collective-permute-start(bf16[32,64,128]{2,1,0:T(8,128)(2,1)} %get-tuple-element.34), channel_id=1, source_target_pairs={{0,1},{1,0},{2,3},{3,2},{4,5},{5,4},{6,7},{7,6},{8,9},{9,8},{10,11... | collective-permute-start | bytes 1572872 | tf_op jit(solution)/shard_map/ppermute | solution.py:16
  502.9 35.6 %collective-permute-start.18 = (bf16[32,64,128]{2,1,0:T(8,128)(2,1)}, bf16[32,64,128]{2,1,0:T(8,128)(2,1)S(1)}, u32[]{:S(2)}, u32[]{:S(2)}) collective-permute-start(bf16[32,64,128]{2,1,0:T(8,128)(2,1)} %get-tuple-element.35), channel_id=1, source_target_pairs={{0,2},{1,3},{2,0},{3,1},{4,6},{5,7},{6,4},{7,5},{8,10},{9,11},{10,... | collective-permute-start | bytes 1572872 | tf_op jit(solution)/shard_map/ppermute | solution.py:16
  506.1 43.8 %collective-permute-start.19 = (bf16[32,64,128]{2,1,0:T(8,128)(2,1)}, bf16[32,64,128]{2,1,0:T(8,128)(2,1)}, u32[]{:S(2)}, u32[]{:S(2)}) collective-permute-start(bf16[32,64,128]{2,1,0:T(8,128)(2,1)} %get-tuple-element.36), channel_id=1, source_target_pairs={{0,3},{1,2},{2,1},{3,0},{4,7},{5,6},{6,5},{7,4},{8,11},{9,10},{10,... | collective-permute-start | bytes 1572872 | tf_op jit(solution)/shard_map/ppermute | solution.py:16
  (27 other events, 577.2 us)
